TPU v7x, 1024 devices: a whole 8x8x8 slice. The times are simulated.
1024 devices in a mesh: dp: 32 (over y, z_lo), expert: 32 (over x, z_hi, core).
Axes of the slice: x: 8, y: 8, z: 8 (z_hi: 2, z_lo: 4; z = z_hi * 4 + z_lo), core: 2. Of those that a mesh axis runs over, the one named last changes fastest.
Arguments:
- tokens: bfloat16 [131072, 3584], P(('dp', 'expert')), may hold values from -6 to 6
- routes: int32 [131072, 1], P(('dp', 'expert')), may hold values from 0 to 31; in each aligned block of 128 rows (0 to 127, 128 to 255, ...) at most 6 rows name the same one
- gates: float32 [131072, 1], P(('dp', 'expert')), may hold values from 0.1 to 1
- counts: int32 [1024], P(('dp', 'expert')), may hold values from 16 to 128, as said below
- expert_weight: bfloat16 [32, 3584, 1024], P('expert'), may hold values from -0.09375 to 0.09375
- cotangent: bfloat16 [131072, 1024], P(('dp', 'expert')), may hold values from -6 to 6
Outputs:
- mixed: bfloat16 [131072, 1024], P(('dp', 'expert'))
- token_grad: bfloat16 [131072, 3584], P(('dp', 'expert'))
- gate_grad: float32 [131072, 1], P(('dp', 'expert'))
Inputs may be any that keep to these rules, and one draw needn't show every extreme that they name: `routes`: among the tokens of one device at most 6 name one expert; some device sends exactly 6 to some expert; every expert is named. The first counts[i] tokens of device i are valid; some device has all of its tokens valid.
All inputs are finite; a program needn't handle non-finite values.
Results may differ from a plain program's by a relative error of at most 0.0058.
Values may be sent and summed in bfloat16 or wider, within the bound.
No kernel may reach another device: no remote copies, remote signals or barrier semaphores. Data moves between devices by JAX's collectives and lax.ppermute only.
A program may use at most 32 MiB of HBM per device.

v0:
```python
import jax
import jax.numpy as jnp
from jax import lax
from jax.sharding import PartitionSpec as P


def forward_rows(inputs, weight):
    pre = jnp.einsum("skd,dh->skh", inputs, weight, preferred_element_type=jnp.float32)
    sig = jax.nn.sigmoid(pre)
    act = (pre * sig).astype(jnp.bfloat16)
    slope = sig * (1.0 + pre * (1.0 - sig))
    return (act, slope)


def backward_rows(upstream, slope, weight):
    delta = (upstream.astype(jnp.float32) * slope).astype(jnp.bfloat16)
    return jnp.einsum("skh,dh->skd", delta, weight, preferred_element_type=jnp.float32).astype(
        jnp.bfloat16
    )


def shards(tokens, routes, gates, counts, expert_weight, cotangent):
    local_rows = tokens.shape[0]
    experts_here = lax.axis_size("expert")
    capacity = 3 * local_rows // (2 * experts_here)
    slots_all = experts_here * capacity
    route = routes[:, 0]
    gate = gates[:, 0]
    weight = expert_weight[0]
    choose = (route[:, None] == jnp.arange(experts_here, dtype=jnp.int32)[None, :]).astype(
        jnp.int32
    )
    running = jnp.cumsum(choose, axis=0)
    rank = jnp.sum(running * choose, axis=1) - 1
    target = route * capacity + rank
    placing = (jnp.arange(slots_all, dtype=jnp.int32)[:, None] == target[None, :]).astype(
        jnp.bfloat16
    )
    position = jnp.arange(local_rows, dtype=jnp.int32)
    valid = (position < counts[0]).astype(jnp.float32)
    total = lax.psum(counts.astype(jnp.float32), ("dp", "expert"))[0]
    scale = jnp.float32(local_rows * lax.axis_size("dp") * experts_here) / total
    factor = valid * scale
    upstream = ((gate * factor)[:, None] * cotangent.astype(jnp.float32)).astype(jnp.bfloat16)
    outgoing = jnp.dot(placing, tokens, preferred_element_type=jnp.float32).astype(jnp.bfloat16)
    outgoing = outgoing.reshape(experts_here, capacity, tokens.shape[1])
    sending = jnp.dot(placing, upstream, preferred_element_type=jnp.float32).astype(jnp.bfloat16)
    sending = sending.reshape(experts_here, capacity, upstream.shape[1])
    act_slots, slope_slots = forward_rows(
        lax.all_to_all(outgoing, "expert", split_axis=0, concat_axis=0, tiled=True), weight
    )
    act_home = lax.all_to_all(act_slots, "expert", split_axis=0, concat_axis=0, tiled=True)
    arrived = lax.all_to_all(sending, "expert", split_axis=0, concat_axis=0, tiled=True)
    grad_slots = backward_rows(arrived, slope_slots, weight)
    grad_home = lax.all_to_all(grad_slots, "expert", split_axis=0, concat_axis=0, tiled=True)
    unplace = (((0,), (0,)), ((), ()))
    act_flat = act_home.reshape(slots_all, act_home.shape[2])
    grad_flat = grad_home.reshape(slots_all, grad_home.shape[2])
    act_float = lax.dot_general(placing, act_flat, unplace, preferred_element_type=jnp.float32)
    token_grad = lax.dot_general(
        placing, grad_flat, unplace, preferred_element_type=jnp.float32
    ).astype(jnp.bfloat16)
    mixed = (gate[:, None] * act_float).astype(jnp.bfloat16)
    gate_grad = (jnp.sum(act_float * cotangent.astype(jnp.float32), axis=1) * factor)[:, None]
    return (mixed, token_grad, gate_grad)


def solution(mesh):
    placed = (
        P(("dp", "expert"), None),
        P(("dp", "expert"), None),
        P(("dp", "expert"), None),
        P(("dp", "expert")),
        P("expert", None, None),
        P(("dp", "expert"), None),
    )
    return jax.shard_map(
        shards,
        mesh=mesh,
        in_specs=placed,
        out_specs=(P(("dp", "expert"), None), P(("dp", "expert"), None), P(("dp", "expert"), None)),
        check_vma=False,
    )
```

profile of v0, /device:TPU:1, one launch (start us, length us, event | category | flops | bytes accessed | tf_op | source)
XLA Modules:
  0.0 291.1 jit_solution(4507127488560204077)
XLA Ops:
  0.6 0.0 copy-start
  0.6 0.8 fusion.15
  1.5 0.2 reduce_window_sum.11
  1.6 0.8 select_reduce_fusion
  2.5 0.7 add_add_fusion
  3.1 0.0 copy-done
  3.1 0.5 convolution_convert_fusion
  3.6 1.5 reshape.47
  5.2 20.6 %all-to-all-start = ((bf16[32,6,3584]{2,1,0:T(8,128)(2,1)}), bf16[32,6,3584]{2,1,0:T(8,128)(2,1)S(1)}, u32[]{:S(2)}, u32[]{:S(2)}) async-start(bf16[32,6,3584]{2,1,0:T(8,128)(2,1)} %reshape.47), calls=%async_computation | async-start | bytes 3670016 | tf_op jit(solution)/shard_map/all_to_all | solution.py:50
  26.4 155.3 %psum.7 = f32[1]{0:T(128)} all-reduce(f32[1]{0:T(128)S(6)} %convert_element_type.43), channel_id=1, replica_groups=mesh['dp'=32,'expert'=32] {'dp','expert'}, use_global_device_ids=true, to_apply=%region_2.3 | all-reduce | flops 1 | bytes 8 | tf_op jit(solution)/shard_map/psum | solution.py:41
  182.4 0.0 copy-done.3
  182.4 0.0 copy-done.1
  182.4 0.3 convolution_convert_fusion.2
  182.8 0.9 reshape.49
  183.7 0.0 all-to-all-done
  183.7 5.6 %all-to-all-start.2 = ((bf16[32,6,1024]{2,1,0:T(8,128)(2,1)}), bf16[32,6,1024]{2,1,0:T(8,128)(2,1)S(1)}, u32[]{:S(2)}, u32[]{:S(2)}) async-start(bf16[32,6,1024]{2,1,0:T(8,128)(2,1)} %reshape.49), calls=%async_computation.2 | async-start | bytes 1048576 | tf_op jit(solution)/shard_map/all_to_all | solution.py:53
  189.4 5.6 %multiply_convert_fusion.1 = (bf16[32,6,1024]{2,0,1:T(8,128)(2,1)S(1)}, f32[32,6,1024]{2,0,1:T(8,128)}) fusion(bf16[1,3584,1024]{2,1,0:T(8,128)(2,1)} %param.10, bf16[32,6,3584]{2,1,0:T(8,128)(2,1)S(1)} %all-to-all-done), kind=kOutput, calls=%fused_computation.10 | convolution fusion | flops 1410269184 | bytes 9895936 | tf_op jit(solution)/shard_map/skd,dh->skh/dot_general | solution.py:8
  195.0 1.0 copy.15
  196.0 12.2 %all-to-all-done.2 = bf16[32,6,1024]{2,1,0:T(8,128)(2,1)S(1)} async-done(((bf16[32,6,1024]{2,1,0:T(8,128)(2,1)}), bf16[32,6,1024]{2,1,0:T(8,128)(2,1)S(1)}, u32[]{:S(2)}, u32[]{:S(2)}) %all-to-all-start.2) | async-done | bytes 393248 | tf_op jit(solution)/shard_map/all_to_all | solution.py:53
  208.2 0.8 copy-done.2
  209.0 6.2 %all-to-all-start.1 = ((bf16[32,6,1024]{2,1,0:T(8,128)(2,1)}), bf16[32,6,1024]{2,1,0:T(8,128)(2,1)S(1)}, u32[]{:S(2)}, u32[]{:S(2)}) async-start(bf16[32,6,1024]{2,1,0:T(8,128)(2,1)} %copy.15), calls=%async_computation.1 | async-start | bytes 1048576 | tf_op jit(solution)/shard_map/all_to_all | solution.py:52
  215.2 0.0 copy-done.4
  215.3 6.0 %fusion.4 = bf16[32,6,3584]{2,0,1:T(8,128)(2,1)S(1)} fusion(bf16[1,3584,1024]{2,1,0:T(8,128)(2,1)} %param.10, f32[32,6,1024]{2,0,1:T(8,128)S(1)} %copy-done.4, bf16[32,6,1024]{2,1,0:T(8,128)(2,1)} %copy-done.2), kind=kOutput, calls=%fused_computation.4 | convolution fusion | flops 1411940352 | bytes 9895936 | tf_op jit(solution)/shard_map/skh,dh->skd/dot_general | solution.py:17
  221.3 2.0 copy.17
  223.3 10.8 %all-to-all-done.1 = bf16[32,6,1024]{2,1,0:T(8,128)(2,1)S(1)} async-done(((bf16[32,6,1024]{2,1,0:T(8,128)(2,1)}), bf16[32,6,1024]{2,1,0:T(8,128)(2,1)S(1)}, u32[]{:S(2)}, u32[]{:S(2)}) %all-to-all-start.1) | async-done | bytes 393248 | tf_op jit(solution)/shard_map/all_to_all | solution.py:52
  234.1 6.2 %all-to-all-start.3 = ((bf16[32,6,3584]{2,1,0:T(8,128)(2,1)}), bf16[32,6,3584]{2,1,0:T(8,128)(2,1)S(1)}, u32[]{:S(2)}, u32[]{:S(2)}) async-start(bf16[32,6,3584]{2,1,0:T(8,128)(2,1)} %copy.17), calls=%async_computation.3 | async-start | bytes 3670016 | tf_op jit(solution)/shard_map/all_to_all | solution.py:55
  240.3 0.9 reshape.48
  241.2 2.1 fusion.9
  243.3 0.5 bitcast_multiply_fusion
  243.8 43.3 %all-to-all-done.3 = bf16[32,6,3584]{2,1,0:T(8,128)(2,1)S(1)} async-done(((bf16[32,6,3584]{2,1,0:T(8,128)(2,1)}), bf16[32,6,3584]{2,1,0:T(8,128)(2,1)S(1)}, u32[]{:S(2)}, u32[]{:S(2)}) %all-to-all-start.3) | async-done | bytes 1376288 | tf_op jit(solution)/shard_map/all_to_all | solution.py:55
  287.1 1.3 reshape.50
  288.4 2.7 convolution_convert_fusion.1
  (5 shorter events, 0.0 us)
Async XLA Ops:
  0.6 2.5 copy-start
  5.1 177.2 %copy-start.3 = (f32[128,1]{0,1:T(1,128)S(1)}, f32[128,1]{0,1:T(1,128)}, u32[]{:S(2)}) copy-start(f32[128,1]{0,1:T(1,128)} %param.8) | copy-start | bytes 1540
  5.1 177.3 %copy-start.1 = (bf16[128,1024]{1,0:T(8,128)(2,1)S(1)}, bf16[128,1024]{1,0:T(8,128)(2,1)}, u32[]{:S(2)}) copy-start(bf16[128,1024]{1,0:T(8,128)(2,1)} %param.11) | copy-start | bytes 786436
  5.2 178.6 %all-to-all-start = ((bf16[32,6,3584]{2,1,0:T(8,128)(2,1)}), bf16[32,6,3584]{2,1,0:T(8,128)(2,1)S(1)}, u32[]{:S(2)}, u32[]{:S(2)}) async-start(bf16[32,6,3584]{2,1,0:T(8,128)(2,1)} %reshape.47), calls=%async_computation | async-start | bytes 3670016 | tf_op jit(solution)/shard_map/all_to_all | solution.py:50
  183.7 24.5 %all-to-all-start.2 = ((bf16[32,6,1024]{2,1,0:T(8,128)(2,1)}), bf16[32,6,1024]{2,1,0:T(8,128)(2,1)S(1)}, u32[]{:S(2)}, u32[]{:S(2)}) async-start(bf16[32,6,1024]{2,1,0:T(8,128)(2,1)} %reshape.49), calls=%async_computation.2 | async-start | bytes 1048576 | tf_op jit(solution)/shard_map/all_to_all | solution.py:53
  195.0 20.3 %copy-start.4 = (f32[32,6,1024]{2,0,1:T(8,128)S(1)}, f32[32,6,1024]{2,0,1:T(8,128)}, u32[]{:S(2)}) copy-start(f32[32,6,1024]{2,0,1:T(8,128)} %get-tuple-element.6) | copy-start | bytes 2359300
  208.2 0.8 copy-start.2
  209.0 25.1 %all-to-all-start.1 = ((bf16[32,6,1024]{2,1,0:T(8,128)(2,1)}), bf16[32,6,1024]{2,1,0:T(8,128)(2,1)S(1)}, u32[]{:S(2)}, u32[]{:S(2)}) async-start(bf16[32,6,1024]{2,1,0:T(8,128)(2,1)} %copy.15), calls=%async_computation.1 | async-start | bytes 1048576 | tf_op jit(solution)/shard_map/all_to_all | solution.py:52
  234.1 53.0 %all-to-all-start.3 = ((bf16[32,6,3584]{2,1,0:T(8,128)(2,1)}), bf16[32,6,3584]{2,1,0:T(8,128)(2,1)S(1)}, u32[]{:S(2)}, u32[]{:S(2)}) async-start(bf16[32,6,3584]{2,1,0:T(8,128)(2,1)} %copy.17), calls=%async_computation.3 | async-start | bytes 3670016 | tf_op jit(solution)/shard_map/all_to_all | solution.py:55
where the time goes:
time: 294 us; the launch traced here: 291 us
  blocking collectives  155 us (53%)
  waiting for transfers between devices  66.2 us (23%)
  starting transfers between devices  38.7 us (13%)
  matrix products  17.3 us (6%)
  local copies, waits for them, and re-layouts  8.49 us (3%)
  other arithmetic  3 us (1%)
    psum x1, blocking collectives, shards(): total = lax.psum(counts.astype(jnp.float32), ('dp', 'expert'))[0]  155 us
    all_to_all x1, waiting for transfers between devices, shards(): lax.all_to_all(grad_slots, 'expert', split_axis=0, concat_axis=0, tiled=T...  43.3 us
    all_to_all x1, starting transfers between devices, shards(): lax.all_to_all(outgoing, 'expert', split_axis=0, concat_axis=0, tiled=True)  20.6 us
    all_to_all x1, waiting for transfers between devices, shards(): lax.all_to_all(sending, 'expert', split_axis=0, concat_axis=0, tiled=True)  12.2 us
    all_to_all x1, waiting for transfers between devices, shards(): lax.all_to_all(act_slots, 'expert', split_axis=0, concat_axis=0, tiled=True)  10.8 us
    all_to_all x1, starting transfers between devices, shards(): lax.all_to_all(grad_slots, 'expert', split_axis=0, concat_axis=0, tiled=T...  6.23 us
    all_to_all x1, starting transfers between devices, shards(): lax.all_to_all(act_slots, 'expert', split_axis=0, concat_axis=0, tiled=True)  6.23 us
    dot_general x1, matrix products, backward_rows(): jnp.einsum('skh,dh->skd', delta, weight, preferred_element_type=jnp.float32)  6.05 us
  transfers between devices with their start and end apart: 4, of which 3 were waited for; matrix products, arithmetic and copies ran while one was open for 7% of the time, Pallas kernels for 0%

commit v1 on v0

v1 whole, which is shorter than its diff:
```python
import functools

import jax
import jax.numpy as jnp
from jax import lax
from jax.experimental import pallas as pl
from jax.experimental.pallas import tpu as pltpu
from jax.sharding import Mesh, PartitionSpec as P

ROWS = 8
SLOTS = 6
PARTS = 3

BF = jnp.bfloat16
F32 = jnp.float32


def dot(a, b, dims=(((1,), (0,)), ((), ()))):
    return lax.dot_general(a, b, dims, preferred_element_type=F32)


def iota(shape, axis):
    return lax.broadcasted_iota(jnp.int32, shape, axis)


def places(route, experts):
    tokens = route.shape[1]
    choose = (iota((experts, tokens), 0) == route).astype(F32)
    before = (iota((tokens, tokens), 0) < iota((tokens, tokens), 1)).astype(BF)
    rank = jnp.sum(dot(choose.astype(BF), before) * choose, axis=0, keepdims=True).astype(jnp.int32)
    late = (rank >= PARTS).astype(jnp.int32)
    part = rank - PARTS * late
    row = iota((experts * ROWS, tokens), 0)
    main = row == route * ROWS + rank
    tail = row == route * ROWS + (SLOTS + late)
    return main, [jnp.logical_and(tail, part == i) for i in range(PARTS)]


def column(row):
    n = row.shape[1]
    return jnp.sum(jnp.where(iota((n, n), 0) == iota((n, n), 1), row, 0.0), axis=1, keepdims=True)


def line(col):
    n = col.shape[0]
    return jnp.sum(jnp.where(iota((n, n), 0) == iota((n, n), 1), col, 0.0), axis=0, keepdims=True)


def slot_part(rows, part, axis):
    slot, tail = iota((rows, rows), axis), iota((rows, rows), 1 - axis)
    inner = jnp.bitwise_and(tail, ROWS - 1)
    want = tail - inner + PARTS * (inner - SLOTS) + part
    return jnp.logical_and(inner >= SLOTS, slot == want).astype(BF)


def pack_kernel(count, route, gate, tokens, cotangent, out):
    experts = out.shape[0] // ROWS
    main, tails = places(route[...], experts)
    local = route.shape[1]
    weight = jnp.where(iota((1, local), 1) < count[0], gate[...], 0.0)
    main = main.astype(BF)
    width = out.shape[1] // PARTS
    wide = out.shape[1]
    for i in range(PARTS):
        place = tails[i].astype(BF)
        factor = jnp.sum(jnp.where(tails[i], weight, 0.0), axis=1, keepdims=True)
        rest = jnp.concatenate(
            [dot(place, tokens[:, wide:]), dot(place, cotangent[...]) * factor], axis=1
        )
        body = dot(main, tokens[:, i * width : (i + 1) * width])
        out[:, i * width : (i + 1) * width] = (body + rest).astype(BF)


def expert_kernel(scale, data, weight, out):
    rows, wide = data.shape
    width = wide // PARTS
    tail = weight.shape[0] - wide
    rest = dot(slot_part(rows, 0, 0), data[:, :width])
    for i in range(1, PARTS):
        rest = rest + dot(slot_part(rows, i, 0), data[:, i * width : (i + 1) * width])
    pre = dot(data[...], weight[:wide, :]) + dot(rest[:, :tail].astype(BF), weight[wide:, :])
    sig = 1.0 / (1.0 + jnp.exp(-pre))
    act = (pre * sig).astype(BF)
    slope = sig * (1.0 + pre * (1.0 - sig))
    delta = (rest[:, tail:] * slope).astype(BF)
    turned = (((1,), (1,)), ((), ()))
    last = (dot(delta, weight[wide:, :], turned) * scale[0]).astype(BF)
    home = jnp.concatenate([last, act], axis=1)
    for i in range(PARTS):
        cols = slice(i * width, (i + 1) * width)
        grad = dot(delta, weight[cols, :], turned) * scale[0]
        out[:, cols] = (grad + dot(slot_part(rows, i, 1), home)).astype(BF)


def unpack_kernel(count, scale, route, gate, data, cotangent, mixed, token_grad, gate_grad):
    experts = data.shape[0] // ROWS
    main, tails = places(route[...], experts)
    local = route.shape[1]
    wide = data.shape[1]
    width = wide // PARTS
    turned = (((0,), (0,)), ((), ()))
    main = main.astype(BF)
    rest = None
    for i in range(PARTS):
        cols = slice(i * width, (i + 1) * width)
        token_grad[:, cols] = dot(main, data[:, cols], turned).astype(BF)
        more = dot(tails[i].astype(BF), data[:, cols], turned)
        rest = more if rest is None else rest + more
    tail = token_grad.shape[1] - wide
    token_grad[:, wide:] = rest[:, :tail].astype(BF)
    act = rest[:, tail:]
    mixed[...] = (column(gate[...]) * act).astype(BF)
    total = jnp.sum(act * cotangent[...].astype(F32), axis=1, keepdims=True)
    factor = jnp.where(iota((1, local), 1) < count[0], scale[0], 0.0)
    gate_grad[...] = line(total) * factor


VM = pl.BlockSpec(memory_space=pltpu.VMEM)
SM = pl.BlockSpec(memory_space=pltpu.SMEM)


def call(kernel, ins, outs, name, flops):
    return pl.pallas_call(
        kernel,
        in_specs=ins,
        out_specs=[VM] * len(outs) if isinstance(outs, list) else VM,
        out_shape=outs,
        name=name,
        cost_estimate=pl.CostEstimate(flops=flops, bytes_accessed=10_000_000, transcendentals=0),
        compiler_params=pltpu.CompilerParams(vmem_limit_bytes=48 << 20),
    )


def shards(tokens, routes, gates, counts, expert_weight, cotangent):
    local, deep = tokens.shape
    units = cotangent.shape[1]
    experts = lax.axis_size("x") * lax.axis_size("zh") * lax.axis_size("core")
    devices = experts * lax.axis_size("y") * lax.axis_size("zl")
    group = ("x", "zh", "core")
    rows = experts * ROWS
    wide = (deep + units) * SLOTS // ROWS
    route = routes.reshape(1, local)
    gate = gates.reshape(1, local)
    weight = expert_weight[0]
    payload = call(
        pack_kernel,
        [SM, VM, VM, VM, VM],
        jax.ShapeDtypeStruct((rows, wide), BF),
        "pack",
        2 * rows * local * 2 * wide,
    )(counts, route, gate, tokens, cotangent)
    arrived = lax.all_to_all(
        payload.reshape(experts, ROWS, wide), group, split_axis=0, concat_axis=0, tiled=True
    )
    total = counts.astype(F32)
    for axis in ("y", ("zh", "zl"), "x", "core"):
        total = lax.psum(total, axis)
    scale = jnp.float32(local * devices) / total
    back = call(
        expert_kernel,
        [SM, VM, VM],
        jax.ShapeDtypeStruct((rows, wide), BF),
        "expert",
        4 * rows * deep * units,
    )(scale, arrived.reshape(rows, wide), weight)
    home = lax.all_to_all(
        back.reshape(experts, ROWS, wide), group, split_axis=0, concat_axis=0, tiled=True
    )
    mixed, token_grad, gate_grad = call(
        unpack_kernel,
        [SM, SM, VM, VM, VM, VM],
        [
            jax.ShapeDtypeStruct((local, units), BF),
            jax.ShapeDtypeStruct((local, deep), BF),
            jax.ShapeDtypeStruct((1, local), F32),
        ],
        "unpack",
        2 * rows * local * 2 * wide,
    )(counts, scale, route, gate, home.reshape(rows, wide), cotangent)
    return (mixed, token_grad, gate_grad.reshape(local, 1))


def solution(mesh):
    fine = Mesh(mesh.devices.reshape(8, 4, 8, 2, 2), ("y", "zl", "x", "zh", "core"))
    every = ("y", "zl", "x", "zh", "core")
    placed = (
        P(every, None),
        P(every, None),
        P(every, None),
        P(every),
        P(("x", "zh", "core"), None, None),
        P(every, None),
    )
    return jax.shard_map(
        shards,
        mesh=fine,
        in_specs=placed,
        out_specs=(P(every, None), P(every, None), P(every, None)),
        check_vma=False,
    )
```

time: 294 us -> 166 us (0.56)
  waiting for transfers between devices: 66.2 us -> 0.01 us
  blocking collectives: 155 us -> 126 us
  starting transfers between devices: 38.7 us -> 20.5 us
  matrix products: 17.3 us -> 0 us
  Pallas kernels: 0 us -> 13 us
  local copies, waits for them, and re-layouts: 8.49 us -> 3.45 us
  other arithmetic: 3 us -> 0 us
    psum x1 -> x4, blocking collectives: 155 us -> 74.5 us  [shards(): total = lax.psum(total, axis)]
    all_to_all x4 -> x1, waiting for transfers between devices: 66.2 us -> 0.01 us  [shards(): lax.all_to_all(payload.reshape(experts, ROWS, wide), group, split_axis=0,...]
    all_to_all x0 -> x1, blocking collectives: none -> 51 us  [shards(): lax.all_to_all(back.reshape(experts, ROWS, wide), group, split_axis=0, co...]
    all_to_all x4 -> x1, starting transfers between devices: 38.7 us -> 20.5 us  [shards(): lax.all_to_all(payload.reshape(experts, ROWS, wide), group, split_axis=0,...]
    dot_general x6 -> x0, matrix products: 17.3 us -> none  [the longest x1 6.05 us: backward_rows(): jnp.einsum('skh,dh->skd', delta, weight, preferred_element_type=jnp.float32)]
    pallas_call x0 -> x3, Pallas kernels: none -> 13 us  [the longest x1 8.63 us: shards(): call(expert_kernel, [SM, VM, VM], jax.ShapeDtypeStruct((rows, wide), BF),...]
    reshape x4 -> x0, local copies, waits for them, and re-layouts: 4.65 us -> none  [the longest x1 1.5 us: shards(): outgoing = outgoing.reshape(experts_here, capacity, tokens.shape[1])]
    convert_element_type x2 -> x0, local copies, waits for them, and re-layouts: 3.03 us -> none  [the longest x1 2.02 us: backward_rows(): jnp.einsum('skh,dh->skd', delta, weight, preferred_element_type=jnp.float32)]
  transfers between devices with their start and end apart: 4 -> 1, of which waited for: 3 -> 0; matrix products, arithmetic and copies ran while one was open for 7% -> 0% of each run, Pallas kernels for 0% -> 0%
where the time goes in v1:
time: 166 us; the launch traced here: 164 us
  blocking collectives  126 us (76%)
  starting transfers between devices  20.5 us (12%)
  Pallas kernels  13 us (8%)
  local copies, waits for them, and re-layouts  3.45 us (2%)
  between operations  2.03 us (1%)
    psum x4, blocking collectives, shards(): total = lax.psum(total, axis)  74.5 us
    all_to_all x1, blocking collectives, shards(): lax.all_to_all(back.reshape(experts, ROWS, wide), group, split_axis=0, co...  51 us
    all_to_all x1, starting transfers between devices, shards(): lax.all_to_all(payload.reshape(experts, ROWS, wide), group, split_axis=0,...  20.5 us
    pallas_call x1, Pallas kernels, shards(): call(expert_kernel, [SM, VM, VM], jax.ShapeDtypeStruct((rows, wide), BF),...  8.63 us
    unnamed x14, local copies, waits for them, and re-layouts  3.45 us
  transfers between devices with their start and end apart: 1, of which 0 were waited for; matrix products, arithmetic and copies ran while one was open for 0% of the time, Pallas kernels for 0%

profile of v1, /device:TPU:1, one launch (start us, length us, event | category | flops | bytes accessed | tf_op | source)
XLA Modules:
  0.0 164.5 jit_solution(13297188194629198841)
XLA Ops:
  1.3 0.0 copy-start
  1.3 0.9 copy-done
  2.2 0.0 copy-start.2
  2.2 1.2 copy-done.2
  3.4 0.0 copy-start.3
  3.4 0.7 copy-done.3
  4.1 0.0 copy-start.5
  4.1 0.7 copy-done.5
  4.7 2.5 %pack.1 = bf16[256,3456]{1,0:T(8,128)(2,1)} custom-call(s32[1]{0:T(128)S(6)} %copy.9.count, s32[1,128]{1,0:T(1,128)S(1)} %bitcast.11, f32[1,128]{1,0:T(1,128)S(1)} %bitcast.13, bf16[128,3584]{1,0:T(8,128)(2,1)S(1)} %copy-done.2, bf16[128,1024]{1,0:T(8,128)(2,1)S(1)} %copy-done), custom_call_target="tpu_custom_call" | custom-call | flops 452984832 | bytes 10000000 | tf_op jit(solution)/shard_map/pack/pallas_call | solution.py:145
  7.2 20.5 %all-to-all-start = ((bf16[32,8,3456]{2,1,0:T(8,128)(2,1)}), bf16[32,8,3456]{2,1,0:T(8,128)(2,1)S(1)}, u32[]{:S(2)}, u32[]{:S(2)}) async-start(bf16[32,8,3456]{2,1,0:T(8,128)(2,1)} %bitcast.2), calls=%async_computation | async-start | bytes 3538944 | tf_op jit(solution)/shard_map/all_to_all | solution.py:152
  27.7 15.5 %psum.28 = f32[1]{0:T(128)} all-reduce(f32[1]{0:T(128)S(6)} %convert_element_type.3), channel_id=1, replica_groups=mesh['y'=8,'zl'=4,'x'=8,'zh'=2,'core'=2] {'y'}, use_global_device_ids=true, to_apply=%region_0.0 | all-reduce | flops 1 | bytes 8 | tf_op jit(solution)/shard_map/psum | solution.py:157
  43.2 34.1 %psum.29 = f32[1]{0:T(128)} all-reduce(f32[1]{0:T(128)} %psum.28), channel_id=1, replica_groups=mesh['y'=8,'zl'=4,'x'=8,'zh'=2,'core'=2] {'zh','zl'}, use_global_device_ids=true, to_apply=%region_1.0 | all-reduce | flops 1 | bytes 8 | tf_op jit(solution)/shard_map/psum | solution.py:157
  77.2 13.8 %psum.30 = f32[1]{0:T(128)} all-reduce(f32[1]{0:T(128)} %psum.29), channel_id=1, replica_groups=mesh['y'=8,'zl'=4,'x'=8,'zh'=2,'core'=2] {'x'}, use_global_device_ids=true, to_apply=%region_2.0 | all-reduce | flops 1 | bytes 8 | tf_op jit(solution)/shard_map/psum | solution.py:157
  91.0 11.2 %psum.31 = f32[1]{0:T(128)} all-reduce(f32[1]{0:T(128)} %psum.30), channel_id=1, replica_groups=mesh['y'=8,'zl'=4,'x'=8,'zh'=2,'core'=2] {'core'}, use_global_device_ids=true, to_apply=%region_3.0 | all-reduce | flops 1 | bytes 8 | tf_op jit(solution)/shard_map/psum | solution.py:157
  102.9 0.0 all-to-all-done
  102.9 8.6 %expert.1 = bf16[256,3456]{1,0:T(8,128)(2,1)S(1)} custom-call(f32[1]{0:T(128)S(6)} %div.3.scale, bf16[256,3456]{1,0:T(8,128)(2,1)S(1)} %bitcast.9, bf16[3584,1024]{1,0:T(8,128)(2,1)} %bitcast.15), custom_call_target="tpu_custom_call" | custom-call | flops 3758096384 | bytes 10000000 | tf_op jit(solution)/shard_map/expert/pallas_call | solution.py:159
  111.6 0.0 copy-start.1
  111.6 0.0 copy-start.4
  111.6 0.0 copy-start.6
  111.6 51.0 %all_to_all.10 = bf16[32,8,3456]{2,1,0:T(8,128)(2,1)S(1)} all-to-all(bf16[32,8,3456]{2,1,0:T(8,128)(2,1)S(1)} %bitcast.10), channel_id=1, replica_groups=mesh['y'=8,'zl'=4,'x'=8,'zh'=2,'core'=2] {'x','zh','core'}, dimensions={0} | all-to-all | bytes 3538944 | tf_op jit(solution)/shard_map/all_to_all | solution.py:166
  162.6 0.0 copy-done.1
  162.6 0.0 copy-done.4
  162.6 0.0 copy-done.6
  162.6 1.9 %unpack.1 = (bf16[128,1024]{1,0:T(8,128)(2,1)}, bf16[128,3584]{1,0:T(8,128)(2,1)}, f32[1,128]{1,0:T(1,128)}) custom-call(s32[1]{0:T(128)S(6)} %copy.9.count, f32[1]{0:T(128)S(6)} %div.3.scale, s32[1,128]{1,0:T(1,128)S(1)} %bitcast.12, f32[1,128]{1,0:T(1,128)S(1)} %bitcast.14, bf16[256,3456]{1,0:T(8,128)(2,1)S(1)} %bitcast.8, bf16[128,1024]{1,0:T(8,128)(2,1)S(1)} %copy-done.1), custom_call_target="tpu_custom_call" | custom-call | flops 452984832 | bytes 10000000 | tf_op jit(solution)/shard_map/unpack/pallas_call | solution.py:169
Async XLA Ops:
  1.3 1.0 copy-start
  2.2 1.2 copy-start.2
  3.4 0.7 copy-start.3
  4.1 0.7 copy-start.5
  7.2 95.7 %all-to-all-start = ((bf16[32,8,3456]{2,1,0:T(8,128)(2,1)}), bf16[32,8,3456]{2,1,0:T(8,128)(2,1)S(1)}, u32[]{:S(2)}, u32[]{:S(2)}) async-start(bf16[32,8,3456]{2,1,0:T(8,128)(2,1)} %bitcast.2), calls=%async_computation | async-start | bytes 3538944 | tf_op jit(solution)/shard_map/all_to_all | solution.py:152
  111.6 51.0 %copy-start.1 = (bf16[128,1024]{1,0:T(8,128)(2,1)S(1)}, bf16[128,1024]{1,0:T(8,128)(2,1)}, u32[]{:S(2)}) copy-start(bf16[128,1024]{1,0:T(8,128)(2,1)} %cotangent.3) | copy-start | bytes 786436
  111.6 51.0 %copy-start.4 = (s32[128,1]{0,1:T(1,128)S(1)}, s32[128,1]{0,1:T(1,128)}, u32[]{:S(2)}) copy-start(s32[128,1]{0,1:T(1,128)} %param.7) | copy-start | bytes 1540
  111.6 51.0 %copy-start.6 = (f32[128,1]{0,1:T(1,128)S(1)}, f32[128,1]{0,1:T(1,128)}, u32[]{:S(2)}) copy-start(f32[128,1]{0,1:T(1,128)} %param.8) | copy-start | bytes 1540

commit v2 on v1

--- a/solution.py
+++ b/solution.py
@@ -53,42 +53,89 @@
     return jnp.logical_and(inner >= SLOTS, slot == want).astype(BF)
 
 
-def pack_kernel(count, route, gate, tokens, cotangent, out):
-    experts = out.shape[0] // ROWS
-    main, tails = places(route[...], experts)
-    local = route.shape[1]
+def pack_kernel(count, route_in, gate_in, tokens_in, cotangent_in, out_hbm, route, gate, tokens, cotangent, out, sems):
+    local, deep = tokens.shape
+    wide = out.shape[1]
+    width = wide // PARTS
+    edges = [i * width for i in range(PARTS)] + [wide, deep]
+
+    def piece(i):
+        cols = pl.ds(edges[i], edges[i + 1] - edges[i])
+        return pltpu.make_async_copy(tokens_in.at[:, cols], tokens.at[:, cols], sems.at[i])
+
+    small = [
+        pltpu.make_async_copy(route_in, route, sems.at[PARTS + 1]),
+        pltpu.make_async_copy(gate_in, gate, sems.at[PARTS + 2]),
+    ]
+    side = pltpu.make_async_copy(cotangent_in, cotangent, sems.at[PARTS + 3])
+    pieces = [piece(i) for i in range(PARTS + 1)]
+    for copy in small + [pieces[PARTS], side] + pieces[:PARTS]:
+        copy.start()
+    for copy in small:
+        copy.wait()
+    main, tails = places(route[...], out.shape[0] // ROWS)
     weight = jnp.where(iota((1, local), 1) < count[0], gate[...], 0.0)
     main = main.astype(BF)
-    width = out.shape[1] // PARTS
-    wide = out.shape[1]
-    for i in range(PARTS):
+    factors = [
+        jnp.sum(jnp.where(tail, weight, 0.0), axis=1, keepdims=True) for tail in tails
+    ]
+    pieces[PARTS].wait()
+    side.wait()
+    sent = []
+    for i in range(PARTS):
+        cols = slice(i * width, (i + 1) * width)
         place = tails[i].astype(BF)
-        factor = jnp.sum(jnp.where(tails[i], weight, 0.0), axis=1, keepdims=True)
         rest = jnp.concatenate(
-            [dot(place, tokens[:, wide:]), dot(place, cotangent[...]) * factor], axis=1
+            [dot(place, tokens[:, wide:]), dot(place, cotangent[...]) * factors[i]], axis=1
         )
-        body = dot(main, tokens[:, i * width : (i + 1) * width])
-        out[:, i * width : (i + 1) * width] = (body + rest).astype(BF)
-
-
-def expert_kernel(scale, data, weight, out):
+        pieces[i].wait()
+        out[:, cols] = (dot(main, tokens[:, cols]) + rest).astype(BF)
+        copy = pltpu.make_async_copy(
+            out.at[:, pl.ds(i * width, width)],
+            out_hbm.at[:, pl.ds(i * width, width)],
+            sems.at[PARTS + 4 + i],
+        )
+        copy.start()
+        sent.append(copy)
+    for copy in sent:
+        copy.wait()
+
+
+def expert_kernel(total, data, weight_in, out, total_out, weight, sems):
+    total_out[0] = total[0]
     rows, wide = data.shape
+    deep = weight.shape[0]
     width = wide // PARTS
-    tail = weight.shape[0] - wide
+    tail = deep - wide
+    edges = [i * width for i in range(PARTS)] + [wide, deep]
+    pieces = [
+        pltpu.make_async_copy(
+            weight_in.at[pl.ds(edges[i], edges[i + 1] - edges[i]), :],
+            weight.at[pl.ds(edges[i], edges[i + 1] - edges[i]), :],
+            sems.at[i],
+        )
+        for i in range(PARTS + 1)
+    ]
+    for i in (PARTS, *range(PARTS)):
+        pieces[i].start()
     rest = dot(slot_part(rows, 0, 0), data[:, :width])
     for i in range(1, PARTS):
         rest = rest + dot(slot_part(rows, i, 0), data[:, i * width : (i + 1) * width])
-    pre = dot(data[...], weight[:wide, :]) + dot(rest[:, :tail].astype(BF), weight[wide:, :])
+    pieces[PARTS].wait()
+    pre = dot(rest[:, :tail].astype(BF), weight[wide:, :])
+    for i in range(PARTS):
+        pieces[i].wait()
+        pre = pre + dot(data[:, i * width : (i + 1) * width], weight[i * width : (i + 1) * width, :])
     sig = 1.0 / (1.0 + jnp.exp(-pre))
     act = (pre * sig).astype(BF)
     slope = sig * (1.0 + pre * (1.0 - sig))
     delta = (rest[:, tail:] * slope).astype(BF)
     turned = (((1,), (1,)), ((), ()))
-    last = (dot(delta, weight[wide:, :], turned) * scale[0]).astype(BF)
+    last = dot(delta, weight[wide:, :], turned).astype(BF)
     home = jnp.concatenate([last, act], axis=1)
     for i in range(PARTS):
         cols = slice(i * width, (i + 1) * width)
-        grad = dot(delta, weight[cols, :], turned) * scale[0]
+        grad = dot(delta, weight[cols, :], turned)
         out[:, cols] = (grad + dot(slot_part(rows, i, 1), home)).astype(BF)
 
 
@@ -103,11 +150,11 @@
     rest = None
     for i in range(PARTS):
         cols = slice(i * width, (i + 1) * width)
-        token_grad[:, cols] = dot(main, data[:, cols], turned).astype(BF)
+        token_grad[:, cols] = (dot(main, data[:, cols], turned) * scale[0]).astype(BF)
         more = dot(tails[i].astype(BF), data[:, cols], turned)
         rest = more if rest is None else rest + more
     tail = token_grad.shape[1] - wide
-    token_grad[:, wide:] = rest[:, :tail].astype(BF)
+    token_grad[:, wide:] = (rest[:, :tail] * scale[0]).astype(BF)
     act = rest[:, tail:]
     mixed[...] = (column(gate[...]) * act).astype(BF)
     total = jnp.sum(act * cotangent[...].astype(F32), axis=1, keepdims=True)
@@ -117,17 +164,19 @@
 
 VM = pl.BlockSpec(memory_space=pltpu.VMEM)
 SM = pl.BlockSpec(memory_space=pltpu.SMEM)
-
-
-def call(kernel, ins, outs, name, flops):
+HB = pl.BlockSpec(memory_space=pltpu.HBM)
+
+
+def call(kernel, ins, outs, shapes, name, flops, scratch=(), room=32 << 20):
     return pl.pallas_call(
         kernel,
         in_specs=ins,
-        out_specs=[VM] * len(outs) if isinstance(outs, list) else VM,
-        out_shape=outs,
+        out_specs=outs,
+        out_shape=shapes,
+        scratch_shapes=scratch,
         name=name,
         cost_estimate=pl.CostEstimate(flops=flops, bytes_accessed=10_000_000, transcendentals=0),
-        compiler_params=pltpu.CompilerParams(vmem_limit_bytes=48 << 20),
+        compiler_params=pltpu.CompilerParams(vmem_limit_bytes=room),
     )
 
 
@@ -144,31 +193,47 @@
     weight = expert_weight[0]
     payload = call(
         pack_kernel,
-        [SM, VM, VM, VM, VM],
+        [SM, HB, HB, HB, HB],
+        HB,
         jax.ShapeDtypeStruct((rows, wide), BF),
         "pack",
         2 * rows * local * 2 * wide,
+        [
+            pltpu.VMEM((1, local), jnp.int32),
+            pltpu.VMEM((1, local), F32),
+            pltpu.VMEM((local, deep), BF),
+            pltpu.VMEM((local, units), BF),
+            pltpu.VMEM((rows, wide), BF),
+            pltpu.SemaphoreType.DMA((2 * PARTS + 4,)),
+        ],
+        room=67_043_328,
     )(counts, route, gate, tokens, cotangent)
     arrived = lax.all_to_all(
         payload.reshape(experts, ROWS, wide), group, split_axis=0, concat_axis=0, tiled=True
     )
     total = counts.astype(F32)
-    for axis in ("y", ("zh", "zl"), "x", "core"):
+    for axis in ("y", "zl", "core"):
+        total = lax.psum(total, axis)
+    back, total = call(
+        expert_kernel,
+        [SM, VM, HB],
+        [VM, SM],
+        [jax.ShapeDtypeStruct((rows, wide), BF), jax.ShapeDtypeStruct((1,), F32)],
+        "expert",
+        4 * rows * deep * units,
+        [pltpu.VMEM((deep, units), BF), pltpu.SemaphoreType.DMA((PARTS + 1,))],
+        room=58 << 20,
+    )(total, arrived.reshape(rows, wide), weight)
+    home = lax.all_to_all(
+        back.reshape(experts, ROWS, wide), group, split_axis=0, concat_axis=0, tiled=True
+    )
+    for axis in ("zh", "x"):
         total = lax.psum(total, axis)
     scale = jnp.float32(local * devices) / total
-    back = call(
-        expert_kernel,
-        [SM, VM, VM],
-        jax.ShapeDtypeStruct((rows, wide), BF),
-        "expert",
-        4 * rows * deep * units,
-    )(scale, arrived.reshape(rows, wide), weight)
-    home = lax.all_to_all(
-        back.reshape(experts, ROWS, wide), group, split_axis=0, concat_axis=0, tiled=True
-    )
     mixed, token_grad, gate_grad = call(
         unpack_kernel,
         [SM, SM, VM, VM, VM, VM],
+        [VM, VM, VM],
         [
             jax.ShapeDtypeStruct((local, units), BF),
             jax.ShapeDtypeStruct((local, deep), BF),

time: 166 us -> 159 us (0.958)
  blocking collectives: 126 us -> 104 us
  starting transfers between devices: 20.5 us -> 32.4 us
  Pallas kernels: 13 us -> 16.6 us
  local copies, waits for them, and re-layouts: 3.45 us -> 1.24 us
    all_to_all x1 -> x0, blocking collectives: 51 us -> none  [shards(): lax.all_to_all(back.reshape(experts, ROWS, wide), group, split_axis=0, co...]
    psum x4 -> x5, blocking collectives: 74.5 us -> 104 us  [shards(): total = lax.psum(total, axis)]
    all_to_all x0 -> x1, starting transfers between devices: none -> 11.9 us  [shards(): lax.all_to_all(back.reshape(experts, ROWS, wide), group, split_axis=0, co...]
    pallas_call x3, Pallas kernels: 13 us -> 16.6 us  [the longest x1 11.2 us: shards(): call(expert_kernel, [SM, VM, HB], [VM, SM], [jax.ShapeDtypeStruct((rows,...]
    unnamed x14 -> x8, local copies, waits for them, and re-layouts: 3.45 us -> 1.24 us
  transfers between devices with their start and end apart: 1 -> 2, of which waited for: 0 -> 0; matrix products, arithmetic and copies ran while one was open for 0% -> 0% of each run, Pallas kernels for 0% -> 0%
where the time goes in v2:
time: 159 us; the launch traced here: 156 us
  blocking collectives  104 us (65%)
  starting transfers between devices  32.4 us (20%)
  Pallas kernels  16.6 us (10%)
  between operations  2.06 us (1%)
    psum x5, blocking collectives, shards(): total = lax.psum(total, axis)  104 us
    all_to_all x1, starting transfers between devices, shards(): lax.all_to_all(payload.reshape(experts, ROWS, wide), group, split_axis=0,...  20.5 us
    all_to_all x1, starting transfers between devices, shards(): lax.all_to_all(back.reshape(experts, ROWS, wide), group, split_axis=0, co...  11.9 us
    pallas_call x1, Pallas kernels, shards(): call(expert_kernel, [SM, VM, HB], [VM, SM], [jax.ShapeDtypeStruct((rows,...  11.2 us
    pallas_call x1, Pallas kernels, shards(): call(pack_kernel, [SM, HB, HB, HB, HB], HB, jax.ShapeDtypeStruct((rows, w...  3.55 us
  transfers between devices with their start and end apart: 2, of which 0 were waited for; matrix products, arithmetic and copies ran while one was open for 0% of the time, Pallas kernels for 0%

profile of v2, /device:TPU:1, one launch (start us, length us, event | category | flops | bytes accessed | tf_op | source)
XLA Modules:
  0.0 156.1 jit_solution(13798702440174366315)
XLA Ops:
  1.3 3.5 %pack.1 = bf16[256,3456]{1,0:T(8,128)(2,1)} custom-call(s32[1]{0:T(128)S(6)} %copy.9.count, s32[1,128]{1,0:T(1,128)} %bitcast.9, f32[1,128]{1,0:T(1,128)} %bitcast.11, bf16[128,3584]{1,0:T(8,128)(2,1)} %tokens_in.1, bf16[128,1024]{1,0:T(8,128)(2,1)} %cotangent.1), custom_call_target="tpu_custom_call" | custom-call | flops 452984832 | bytes 10000000 | tf_op jit(solution)/shard_map/pack/pallas_call | solution.py:194
  4.8 20.5 %all-to-all-start = ((bf16[32,8,3456]{2,1,0:T(8,128)(2,1)}), bf16[32,8,3456]{2,1,0:T(8,128)(2,1)S(1)}, u32[]{:S(2)}, u32[]{:S(2)}) async-start(bf16[32,8,3456]{2,1,0:T(8,128)(2,1)} %bitcast.13), calls=%async_computation | async-start | bytes 3538944 | tf_op jit(solution)/shard_map/all_to_all | solution.py:211
  25.3 15.5 %psum.35 = f32[1]{0:T(128)} all-reduce(f32[1]{0:T(128)S(6)} %convert_element_type.3), channel_id=1, replica_groups=mesh['y'=8,'zl'=4,'x'=8,'zh'=2,'core'=2] {'y'}, use_global_device_ids=true, to_apply=%region_0.0 | all-reduce | flops 1 | bytes 8 | tf_op jit(solution)/shard_map/psum | solution.py:216
  40.8 14.7 %psum.36 = f32[1]{0:T(128)} all-reduce(f32[1]{0:T(128)} %psum.35), channel_id=1, replica_groups=mesh['y'=8,'zl'=4,'x'=8,'zh'=2,'core'=2] {'zl'}, use_global_device_ids=true, to_apply=%region_1.0 | all-reduce | flops 1 | bytes 8 | tf_op jit(solution)/shard_map/psum | solution.py:216
  55.5 19.5 %psum.37.total = f32[1]{0:T(128)} all-reduce(f32[1]{0:T(128)} %psum.36), channel_id=1, replica_groups=mesh['y'=8,'zl'=4,'x'=8,'zh'=2,'core'=2] {'core'}, use_global_device_ids=true, to_apply=%region_2.0 | all-reduce | flops 1 | bytes 8 | tf_op jit(solution)/shard_map/psum | solution.py:216
  74.9 0.0 all-to-all-done
  74.9 0.0 copy-start.3
  74.9 1.2 copy-done.3
  76.2 11.2 %expert.1 = (bf16[256,3456]{1,0:T(8,128)(2,1)}, f32[1]{0:T(128)}) custom-call(f32[1]{0:T(128)} %psum.37.total, bf16[256,3456]{1,0:T(8,128)(2,1)} %bitcast.14, bf16[3584,1024]{1,0:T(8,128)(2,1)} %bitcast.16), custom_call_target="tpu_custom_call" | custom-call | flops 3758096384 | bytes 10000000 | tf_op jit(solution)/shard_map/expert/pallas_call | solution.py:217
  87.3 0.0 copy-start
  87.3 0.0 copy-start.1
  87.3 0.0 copy-start.2
  87.4 11.9 %all-to-all-start.1 = ((bf16[32,8,3456]{2,1,0:T(8,128)(2,1)}), bf16[32,8,3456]{2,1,0:T(8,128)(2,1)S(1)}, u32[]{:S(2)}, u32[]{:S(2)}) async-start(bf16[32,8,3456]{2,1,0:T(8,128)(2,1)} %bitcast.15), calls=%async_computation.1 | async-start | bytes 3538944 | tf_op jit(solution)/shard_map/all_to_all | solution.py:227
  99.2 10.8 %psum.38 = f32[1]{0:T(128)} all-reduce(f32[1]{0:T(128)} %get-tuple-element.8), channel_id=1, replica_groups=mesh['y'=8,'zl'=4,'x'=8,'zh'=2,'core'=2] {'zh'}, use_global_device_ids=true, to_apply=%region_3.0 | all-reduce | flops 1 | bytes 8 | tf_op jit(solution)/shard_map/psum | solution.py:231
  110.1 43.5 %psum.39 = f32[1]{0:T(128)} all-reduce(f32[1]{0:T(128)} %psum.38), channel_id=1, replica_groups=mesh['y'=8,'zl'=4,'x'=8,'zh'=2,'core'=2] {'x'}, use_global_device_ids=true, to_apply=%region_4.0 | all-reduce | flops 1 | bytes 8 | tf_op jit(solution)/shard_map/psum | solution.py:231
  154.2 0.0 all-to-all-done.1
  154.2 0.0 copy-done
  154.2 0.0 copy-done.1
  154.3 0.0 copy-done.2
  154.3 1.9 %unpack.1 = (bf16[128,1024]{1,0:T(8,128)(2,1)}, bf16[128,3584]{1,0:T(8,128)(2,1)}, f32[1,128]{1,0:T(1,128)}) custom-call(s32[1]{0:T(128)S(6)} %copy.9.count, f32[1]{0:T(128)S(6)} %div.3.scale, s32[1,128]{1,0:T(1,128)S(1)} %bitcast.10, f32[1,128]{1,0:T(1,128)S(1)} %bitcast.12, bf16[256,3456]{1,0:T(8,128)(2,1)S(1)} %bitcast.8, bf16[128,1024]{1,0:T(8,128)(2,1)S(1)} %copy-done), custom_call_target="tpu_custom_call" | custom-call | flops 452984832 | bytes 10000000 | tf_op jit(solution)/shard_map/unpack/pallas_call | solution.py:233
Async XLA Ops:
  4.8 70.1 %all-to-all-start = ((bf16[32,8,3456]{2,1,0:T(8,128)(2,1)}), bf16[32,8,3456]{2,1,0:T(8,128)(2,1)S(1)}, u32[]{:S(2)}, u32[]{:S(2)}) async-start(bf16[32,8,3456]{2,1,0:T(8,128)(2,1)} %bitcast.13), calls=%async_computation | async-start | bytes 3538944 | tf_op jit(solution)/shard_map/all_to_all | solution.py:211
  74.9 1.2 copy-start.3
  87.3 66.9 %copy-start = (bf16[128,1024]{1,0:T(8,128)(2,1)S(1)}, bf16[128,1024]{1,0:T(8,128)(2,1)}, u32[]{:S(2)}) copy-start(bf16[128,1024]{1,0:T(8,128)(2,1)} %cotangent.1) | copy-start | bytes 786436
  87.3 66.9 %copy-start.1 = (s32[128,1]{0,1:T(1,128)S(1)}, s32[128,1]{0,1:T(1,128)}, u32[]{:S(2)}) copy-start(s32[128,1]{0,1:T(1,128)} %param.7) | copy-start | bytes 1540
  87.3 66.9 %copy-start.2 = (f32[128,1]{0,1:T(1,128)S(1)}, f32[128,1]{0,1:T(1,128)}, u32[]{:S(2)}) copy-start(f32[128,1]{0,1:T(1,128)} %param.8) | copy-start | bytes 1540
  87.4 66.9 %all-to-all-start.1 = ((bf16[32,8,3456]{2,1,0:T(8,128)(2,1)}), bf16[32,8,3456]{2,1,0:T(8,128)(2,1)S(1)}, u32[]{:S(2)}, u32[]{:S(2)}) async-start(bf16[32,8,3456]{2,1,0:T(8,128)(2,1)} %bitcast.15), calls=%async_computation.1 | async-start | bytes 3538944 | tf_op jit(solution)/shard_map/all_to_all | solution.py:227

commit v3 on v2

--- a/solution.py
+++ b/solution.py
@@ -10,6 +10,11 @@
 ROWS = 8
 SLOTS = 6
 PARTS = 3
+STEP = 64.0
+LANES = 128
+CHUNKS = 7
+FLIGHT = 3
+EXPERT_ROOM = 50 << 20
 
 BF = jnp.bfloat16
 F32 = jnp.float32
@@ -101,65 +106,82 @@
         copy.wait()
 
 
-def expert_kernel(total, data, weight_in, out, total_out, weight, sems):
-    total_out[0] = total[0]
+def expert_kernel(total, data, weight_in, out, weight, sems):
     rows, wide = data.shape
     deep = weight.shape[0]
     width = wide // PARTS
     tail = deep - wide
-    edges = [i * width for i in range(PARTS)] + [wide, deep]
+    block = deep // CHUNKS
+    order = [CHUNKS - 1, *range(CHUNKS - 1)]
     pieces = [
         pltpu.make_async_copy(
-            weight_in.at[pl.ds(edges[i], edges[i + 1] - edges[i]), :],
-            weight.at[pl.ds(edges[i], edges[i + 1] - edges[i]), :],
-            sems.at[i],
+            weight_in.at[pl.ds(i * block, block), :], weight.at[pl.ds(i * block, block), :], sems.at[i]
         )
-        for i in range(PARTS + 1)
+        for i in order
     ]
-    for i in (PARTS, *range(PARTS)):
-        pieces[i].start()
+    for piece in pieces[:FLIGHT]:
+        piece.start()
     rest = dot(slot_part(rows, 0, 0), data[:, :width])
     for i in range(1, PARTS):
         rest = rest + dot(slot_part(rows, i, 0), data[:, i * width : (i + 1) * width])
-    pieces[PARTS].wait()
-    pre = dot(rest[:, :tail].astype(BF), weight[wide:, :])
-    for i in range(PARTS):
-        pieces[i].wait()
-        pre = pre + dot(data[:, i * width : (i + 1) * width], weight[i * width : (i + 1) * width, :])
+    pre = None
+    for k, i in enumerate(order):
+        pieces[k].wait()
+        if k + FLIGHT < CHUNKS:
+            pieces[k + FLIGHT].start()
+        left = data[:, i * block : min((i + 1) * block, wide)]
+        if i == CHUNKS - 1:
+            left = jnp.concatenate([left, rest[:, :tail].astype(BF)], axis=1)
+        more = dot(left, weight[i * block : (i + 1) * block, :])
+        pre = more if pre is None else pre + more
     sig = 1.0 / (1.0 + jnp.exp(-pre))
     act = (pre * sig).astype(BF)
     slope = sig * (1.0 + pre * (1.0 - sig))
     delta = (rest[:, tail:] * slope).astype(BF)
     turned = (((1,), (1,)), ((), ()))
-    last = dot(delta, weight[wide:, :], turned).astype(BF)
-    home = jnp.concatenate([last, act], axis=1)
-    for i in range(PARTS):
-        cols = slice(i * width, (i + 1) * width)
-        grad = dot(delta, weight[cols, :], turned)
-        out[:, cols] = (grad + dot(slot_part(rows, i, 1), home)).astype(BF)
-
-
-def unpack_kernel(count, scale, route, gate, data, cotangent, mixed, token_grad, gate_grad):
-    experts = data.shape[0] // ROWS
+    for i in order:
+        start, stop = i * block, min((i + 1) * block, wide)
+        grad = dot(delta, weight[start : start + block, :], turned)
+        if i == CHUNKS - 1:
+            home = jnp.concatenate([grad[:, stop - start :].astype(BF), act], axis=1)
+            for j in range(PARTS):
+                out[:, j * width : (j + 1) * width] = dot(slot_part(rows, j, 1), home).astype(BF)
+        both = grad[:, : stop - start] + out[:, start:stop].astype(F32)
+        out[:, start:stop] = both.astype(BF)
+    high = jnp.floor(total[0] * (1.0 / STEP))
+    lane = iota((rows, LANES), 1)
+    note = jnp.where(lane == 0, high, jnp.where(lane == 1, total[0] - STEP * high, 0.0))
+    out[:, wide:] = note.astype(BF)
+
+
+def unpack_kernel(numerator, count, route, gate, data, cotangent, mixed, token_grad, gate_grad):
+    rows = data.shape[0]
+    experts = rows // ROWS
     main, tails = places(route[...], experts)
     local = route.shape[1]
-    wide = data.shape[1]
+    wide = data.shape[1] - LANES
     width = wide // PARTS
+    lane = iota((rows, LANES), 1)
+    first = jnp.bitwise_and(iota((rows, LANES), 0), ROWS - 1) == 0
+    worth = jnp.where(lane == 0, STEP, jnp.where(lane == 1, 1.0, 0.0))
+    notes = jnp.where(first, data[:, wide:].astype(F32) * worth, 0.0)
+    total = jnp.sum(jnp.sum(notes, axis=0, keepdims=True), axis=1, keepdims=True)
+    scale = numerator / total
     turned = (((0,), (0,)), ((), ()))
     main = main.astype(BF)
     rest = None
     for i in range(PARTS):
         cols = slice(i * width, (i + 1) * width)
-        token_grad[:, cols] = (dot(main, data[:, cols], turned) * scale[0]).astype(BF)
+        token_grad[:, cols] = (dot(main, data[:, cols], turned) * scale).astype(BF)
         more = dot(tails[i].astype(BF), data[:, cols], turned)
         rest = more if rest is None else rest + more
     tail = token_grad.shape[1] - wide
-    token_grad[:, wide:] = (rest[:, :tail] * scale[0]).astype(BF)
+    token_grad[:, wide:] = (rest[:, :tail] * scale).astype(BF)
     act = rest[:, tail:]
     mixed[...] = (column(gate[...]) * act).astype(BF)
-    total = jnp.sum(act * cotangent[...].astype(F32), axis=1, keepdims=True)
-    factor = jnp.where(iota((1, local), 1) < count[0], scale[0], 0.0)
-    gate_grad[...] = line(total) * factor
+    dots = jnp.sum(act * cotangent[...].astype(F32), axis=1, keepdims=True)
+    factor = jnp.where(iota((1, local), 1) < count[0], scale, 0.0)
+    gate_grad[...] = line(dots) * factor
 
 
 VM = pl.BlockSpec(memory_space=pltpu.VMEM)
@@ -211,28 +233,27 @@
     arrived = lax.all_to_all(
         payload.reshape(experts, ROWS, wide), group, split_axis=0, concat_axis=0, tiled=True
     )
-    total = counts.astype(F32)
-    for axis in ("y", "zl", "core"):
-        total = lax.psum(total, axis)
-    back, total = call(
+    total = lax.psum(counts.astype(F32), "y")
+    size, apart = lax.axis_size("zl"), 1
+    while apart < size:
+        total = total + lax.ppermute(total, "zl", [(i, i ^ apart) for i in range(size)])
+        apart = 2 * apart
+    back = call(
         expert_kernel,
         [SM, VM, HB],
-        [VM, SM],
-        [jax.ShapeDtypeStruct((rows, wide), BF), jax.ShapeDtypeStruct((1,), F32)],
+        VM,
+        jax.ShapeDtypeStruct((rows, wide + LANES), BF),
         "expert",
         4 * rows * deep * units,
-        [pltpu.VMEM((deep, units), BF), pltpu.SemaphoreType.DMA((PARTS + 1,))],
-        room=58 << 20,
+        [pltpu.VMEM((deep, units), BF), pltpu.SemaphoreType.DMA((CHUNKS,))],
+        room=EXPERT_ROOM,
     )(total, arrived.reshape(rows, wide), weight)
     home = lax.all_to_all(
-        back.reshape(experts, ROWS, wide), group, split_axis=0, concat_axis=0, tiled=True
-    )
-    for axis in ("zh", "x"):
-        total = lax.psum(total, axis)
-    scale = jnp.float32(local * devices) / total
+        back.reshape(experts, ROWS, wide + LANES), group, split_axis=0, concat_axis=0, tiled=True
+    )
     mixed, token_grad, gate_grad = call(
-        unpack_kernel,
-        [SM, SM, VM, VM, VM, VM],
+        functools.partial(unpack_kernel, float(local * devices)),
+        [SM, VM, VM, VM, VM],
         [VM, VM, VM],
         [
             jax.ShapeDtypeStruct((local, units), BF),
@@ -241,7 +262,7 @@
         ],
         "unpack",
         2 * rows * local * 2 * wide,
-    )(counts, scale, route, gate, home.reshape(rows, wide), cotangent)
+    )(counts, route, gate, home.reshape(rows, wide + LANES), cotangent)
     return (mixed, token_grad, gate_grad.reshape(local, 1))
 
 

time: 159 us -> 140 us (0.88); the launches traced: 156 us -> 140 us
  blocking collectives: 104 us -> 74.3 us
  waiting for transfers between devices: 0.01 us -> 15.4 us
  Pallas kernels: 16.6 us -> 12.8 us
    psum x5 -> x1, blocking collectives: 104 us -> 15.5 us  [shards(): total = lax.psum(counts.astype(F32), 'y')]
    all_to_all x0 -> x1, blocking collectives: none -> 58.9 us  [shards(): lax.all_to_all(back.reshape(experts, ROWS, wide + LANES), group, split_ax...]
    all_to_all x1, waiting for transfers between devices: 0.01 us -> 13.2 us  [shards(): lax.all_to_all(payload.reshape(experts, ROWS, wide), group, split_axis=0,...]
    ppermute x0 -> x2, starting transfers between devices: none -> 13.2 us  [shards(): lax.ppermute(total, 'zl', [(i, i ^ apart) for i in range(size)])]
    all_to_all x1 -> x0, starting transfers between devices: 11.9 us -> none  [shards(): lax.all_to_all(back.reshape(experts, ROWS, wide), group, split_axis=0, co...]
    pallas_call x2, Pallas kernels: 13 us -> 9.23 us  [the longest x1 7.37 us: shards(): call(expert_kernel, [SM, VM, HB], VM, jax.ShapeDtypeStruct((rows, wide +...]
    ppermute x0 -> x2, waiting for transfers between devices: none -> 2.22 us  [shards(): lax.ppermute(total, 'zl', [(i, i ^ apart) for i in range(size)])]
  transfers between devices with their start and end apart: 2 -> 3, of which waited for: 0 -> 3; matrix products, arithmetic and copies ran while one was open for 0% -> 0% of each run, Pallas kernels for 0% -> 0%
where the time goes in v3:
time: 140 us
  blocking collectives  74.3 us (53%)
  starting transfers between devices  33.7 us (24%)
  waiting for transfers between devices  15.4 us (11%)
  Pallas kernels  12.8 us (9%)
  between operations  3.37 us (2%)
    all_to_all x1, blocking collectives, shards(): lax.all_to_all(back.reshape(experts, ROWS, wide + LANES), group, split_ax...  58.9 us
    all_to_all x1, starting transfers between devices, shards(): lax.all_to_all(payload.reshape(experts, ROWS, wide), group, split_axis=0,...  20.5 us
    psum x1, blocking collectives, shards(): total = lax.psum(counts.astype(F32), 'y')  15.5 us
    all_to_all x1, waiting for transfers between devices, shards(): lax.all_to_all(payload.reshape(experts, ROWS, wide), group, split_axis=0,...  13.2 us
    ppermute x2, starting transfers between devices, shards(): lax.ppermute(total, 'zl', [(i, i ^ apart) for i in range(size)])  13.2 us
    pallas_call x1, Pallas kernels, shards(): call(expert_kernel, [SM, VM, HB], VM, jax.ShapeDtypeStruct((rows, wide +...  7.37 us
    pallas_call x1, Pallas kernels, shards(): call(pack_kernel, [SM, HB, HB, HB, HB], HB, jax.ShapeDtypeStruct((rows, w...  3.52 us
  transfers between devices with their start and end apart: 3, of which 3 were waited for; matrix products, arithmetic and copies ran while one was open for 0% of the time, Pallas kernels for 0%

profile of v3, /device:TPU:1, one launch (start us, length us, event | category | flops | bytes accessed | tf_op | source)
XLA Modules:
  0.0 139.5 jit_solution(8701993185155061562)
XLA Ops:
  1.3 3.5 %pack.1 = bf16[256,3456]{1,0:T(8,128)(2,1)} custom-call(s32[1]{0:T(128)S(6)} %copy.9.count, s32[1,128]{1,0:T(1,128)} %bitcast.11, f32[1,128]{1,0:T(1,128)} %bitcast.13, bf16[128,3584]{1,0:T(8,128)(2,1)} %tokens_in.1, bf16[128,1024]{1,0:T(8,128)(2,1)} %cotangent.1), custom_call_target="tpu_custom_call" | custom-call | flops 452984832 | bytes 10000000 | tf_op jit(solution)/shard_map/pack/pallas_call | solution.py:216
  4.8 20.5 %all-to-all-start = ((bf16[32,8,3456]{2,1,0:T(8,128)(2,1)}), bf16[32,8,3456]{2,1,0:T(8,128)(2,1)S(1)}, u32[]{:S(2)}, u32[]{:S(2)}) async-start(bf16[32,8,3456]{2,1,0:T(8,128)(2,1)} %bitcast.15), calls=%async_computation | async-start | bytes 3538944 | tf_op jit(solution)/shard_map/all_to_all | solution.py:233
  25.3 15.5 %psum.7 = f32[1]{0:T(128)} all-reduce(f32[1]{0:T(128)S(6)} %convert_element_type.3), channel_id=1, replica_groups=mesh['y'=8,'zl'=4,'x'=8,'zh'=2,'core'=2] {'y'}, use_global_device_ids=true, to_apply=%region_0.0 | all-reduce | flops 1 | bytes 8 | tf_op jit(solution)/shard_map/psum | solution.py:236
  40.8 4.0 %collective-permute-start = (f32[1]{0:T(128)}, f32[1]{0:T(128)}, u32[]{:S(2)}, u32[]{:S(2)}) collective-permute-start(f32[1]{0:T(128)} %psum.7), channel_id=1, source_target_pairs={{0,32},{32,0},{64,96},{96,64},{1,33},{33,1},{65,97},{97,65},{2,34}... | collective-permute-start | bytes 20 | tf_op jit(solution)/shard_map/ppermute | solution.py:239
  44.8 1.4 %collective-permute-done = f32[1]{0:T(128)} collective-permute-done((f32[1]{0:T(128)}, f32[1]{0:T(128)}, u32[]{:S(2)}, u32[]{:S(2)}) %collective-permute-start) | collective-permute-done | bytes 36 | tf_op jit(solution)/shard_map/ppermute | solution.py:239
  47.5 9.2 %collective-permute-start.1 = (f32[1]{0:T(128)}, f32[1]{0:T(128)}, u32[]{:S(2)}, u32[]{:S(2)}) collective-permute-start(f32[1]{0:T(128)} %add.8), channel_id=1, source_target_pairs={{0,64},{32,96},{64,0},{96,32},{1,65},{33,97},{65,1},{97,33},{2,66}... | collective-permute-start | bytes 20 | tf_op jit(solution)/shard_map/ppermute | solution.py:239
  56.7 0.8 collective-permute-done.1
  58.2 13.2 %all-to-all-done = bf16[32,8,3456]{2,1,0:T(8,128)(2,1)S(1)} async-done(((bf16[32,8,3456]{2,1,0:T(8,128)(2,1)}), bf16[32,8,3456]{2,1,0:T(8,128)(2,1)S(1)}, u32[]{:S(2)}, u32[]{:S(2)}) %all-to-all-start) | async-done | bytes 1769504 | tf_op jit(solution)/shard_map/all_to_all | solution.py:233
  71.4 7.4 %expert.1 = bf16[256,3584]{1,0:T(8,128)(2,1)S(1)} custom-call(f32[1]{0:T(128)S(6)} %add.9.total, bf16[256,3456]{1,0:T(8,128)(2,1)S(1)} %bitcast.10, bf16[3584,1024]{1,0:T(8,128)(2,1)} %bitcast.16), custom_call_target="tpu_custom_call" | custom-call | flops 3758096384 | bytes 10000000 | tf_op jit(solution)/shard_map/expert/pallas_call | solution.py:241
  78.8 0.0 copy-start
  78.8 0.0 copy-start.1
  78.8 0.0 copy-start.2
  78.8 58.9 %all_to_all.10 = bf16[32,8,3584]{2,1,0:T(8,128)(2,1)S(1)} all-to-all(bf16[32,8,3584]{2,1,0:T(8,128)(2,1)S(1)} %bitcast.9), channel_id=1, replica_groups=mesh['y'=8,'zl'=4,'x'=8,'zh'=2,'core'=2] {'x','zh','core'}, dimensions={0} | all-to-all | bytes 3670016 | tf_op jit(solution)/shard_map/all_to_all | solution.py:251
  137.7 0.0 copy-done
  137.7 0.0 copy-done.1
  137.7 0.0 copy-done.2
  137.7 1.9 %unpack.1 = (bf16[128,1024]{1,0:T(8,128)(2,1)}, bf16[128,3584]{1,0:T(8,128)(2,1)}, f32[1,128]{1,0:T(1,128)}) custom-call(s32[1]{0:T(128)S(6)} %copy.9.count, s32[1,128]{1,0:T(1,128)S(1)} %bitcast.12, f32[1,128]{1,0:T(1,128)S(1)} %bitcast.14, bf16[256,3584]{1,0:T(8,128)(2,1)S(1)} %bitcast.8, bf16[128,1024]{1,0:T(8,128)(2,1)S(1)} %copy-done), custom_call_target="tpu_custom_call" | custom-call | flops 452984832 | bytes 10000000 | tf_op jit(solution)/shard_map/unpack/pallas_call | solution.py:254
Async XLA Ops:
  4.8 66.6 %all-to-all-start = ((bf16[32,8,3456]{2,1,0:T(8,128)(2,1)}), bf16[32,8,3456]{2,1,0:T(8,128)(2,1)S(1)}, u32[]{:S(2)}, u32[]{:S(2)}) async-start(bf16[32,8,3456]{2,1,0:T(8,128)(2,1)} %bitcast.15), calls=%async_computation | async-start | bytes 3538944 | tf_op jit(solution)/shard_map/all_to_all | solution.py:233
  40.8 5.4 %collective-permute-start = (f32[1]{0:T(128)}, f32[1]{0:T(128)}, u32[]{:S(2)}, u32[]{:S(2)}) collective-permute-start(f32[1]{0:T(128)} %psum.7), channel_id=1, source_target_pairs={{0,32},{32,0},{64,96},{96,64},{1,33},{33,1},{65,97},{97,65},{2,34}... | collective-permute-start | bytes 20 | tf_op jit(solution)/shard_map/ppermute | solution.py:239
  47.5 10.0 %collective-permute-start.1 = (f32[1]{0:T(128)}, f32[1]{0:T(128)}, u32[]{:S(2)}, u32[]{:S(2)}) collective-permute-start(f32[1]{0:T(128)} %add.8), channel_id=1, source_target_pairs={{0,64},{32,96},{64,0},{96,32},{1,65},{33,97},{65,1},{97,33},{2,66}... | collective-permute-start | bytes 20 | tf_op jit(solution)/shard_map/ppermute | solution.py:239
  78.8 58.9 %copy-start = (bf16[128,1024]{1,0:T(8,128)(2,1)S(1)}, bf16[128,1024]{1,0:T(8,128)(2,1)}, u32[]{:S(2)}) copy-start(bf16[128,1024]{1,0:T(8,128)(2,1)} %cotangent.1) | copy-start | bytes 786436
  78.8 58.9 %copy-start.1 = (s32[128,1]{0,1:T(1,128)S(1)}, s32[128,1]{0,1:T(1,128)}, u32[]{:S(2)}) copy-start(s32[128,1]{0,1:T(1,128)} %param.7) | copy-start | bytes 1540
  78.8 58.9 %copy-start.2 = (f32[128,1]{0,1:T(1,128)S(1)}, f32[128,1]{0,1:T(1,128)}, u32[]{:S(2)}) copy-start(f32[128,1]{0,1:T(1,128)} %param.8) | copy-start | bytes 1540

commit v4 on v3

--- a/solution.py
+++ b/solution.py
@@ -1,5 +1,3 @@
-import functools
-
 import jax
 import jax.numpy as jnp
 from jax import lax
@@ -10,8 +8,6 @@
 ROWS = 8
 SLOTS = 6
 PARTS = 3
-STEP = 64.0
-LANES = 128
 CHUNKS = 7
 FLIGHT = 3
 EXPERT_ROOM = 50 << 20
@@ -106,7 +102,8 @@
         copy.wait()
 
 
-def expert_kernel(total, data, weight_in, out, weight, sems):
+def expert_kernel(total, data, weight_in, out, total_out, weight, sems):
+    total_out[0] = total[0]
     rows, wide = data.shape
     deep = weight.shape[0]
     width = wide // PARTS
@@ -148,25 +145,16 @@
                 out[:, j * width : (j + 1) * width] = dot(slot_part(rows, j, 1), home).astype(BF)
         both = grad[:, : stop - start] + out[:, start:stop].astype(F32)
         out[:, start:stop] = both.astype(BF)
-    high = jnp.floor(total[0] * (1.0 / STEP))
-    lane = iota((rows, LANES), 1)
-    note = jnp.where(lane == 0, high, jnp.where(lane == 1, total[0] - STEP * high, 0.0))
-    out[:, wide:] = note.astype(BF)
-
-
-def unpack_kernel(numerator, count, route, gate, data, cotangent, mixed, token_grad, gate_grad):
+
+
+def unpack_kernel(count, scale_in, route, gate, data, cotangent, mixed, token_grad, gate_grad):
     rows = data.shape[0]
     experts = rows // ROWS
     main, tails = places(route[...], experts)
     local = route.shape[1]
-    wide = data.shape[1] - LANES
+    wide = data.shape[1]
     width = wide // PARTS
-    lane = iota((rows, LANES), 1)
-    first = jnp.bitwise_and(iota((rows, LANES), 0), ROWS - 1) == 0
-    worth = jnp.where(lane == 0, STEP, jnp.where(lane == 1, 1.0, 0.0))
-    notes = jnp.where(first, data[:, wide:].astype(F32) * worth, 0.0)
-    total = jnp.sum(jnp.sum(notes, axis=0, keepdims=True), axis=1, keepdims=True)
-    scale = numerator / total
+    scale = scale_in[0]
     turned = (((0,), (0,)), ((), ()))
     main = main.astype(BF)
     rest = None
@@ -200,6 +188,14 @@
         cost_estimate=pl.CostEstimate(flops=flops, bytes_accessed=10_000_000, transcendentals=0),
         compiler_params=pltpu.CompilerParams(vmem_limit_bytes=room),
     )
+
+
+def both(value, axis):
+    size, apart = lax.axis_size(axis), 1
+    while apart < size:
+        value = value + lax.ppermute(value, axis, [(i, i ^ apart) for i in range(size)])
+        apart = 2 * apart
+    return value
 
 
 def shards(tokens, routes, gates, counts, expert_weight, cotangent):
@@ -233,27 +229,25 @@
     arrived = lax.all_to_all(
         payload.reshape(experts, ROWS, wide), group, split_axis=0, concat_axis=0, tiled=True
     )
-    total = lax.psum(counts.astype(F32), "y")
-    size, apart = lax.axis_size("zl"), 1
-    while apart < size:
-        total = total + lax.ppermute(total, "zl", [(i, i ^ apart) for i in range(size)])
-        apart = 2 * apart
-    back = call(
+    total = both(both(lax.psum(counts.astype(F32), "y"), "zl"), "core")
+    back, total = call(
         expert_kernel,
         [SM, VM, HB],
-        VM,
-        jax.ShapeDtypeStruct((rows, wide + LANES), BF),
+        [VM, SM],
+        [jax.ShapeDtypeStruct((rows, wide), BF), jax.ShapeDtypeStruct((1,), F32)],
         "expert",
         4 * rows * deep * units,
         [pltpu.VMEM((deep, units), BF), pltpu.SemaphoreType.DMA((CHUNKS,))],
         room=EXPERT_ROOM,
     )(total, arrived.reshape(rows, wide), weight)
     home = lax.all_to_all(
-        back.reshape(experts, ROWS, wide + LANES), group, split_axis=0, concat_axis=0, tiled=True
-    )
+        back.reshape(experts, ROWS, wide), group, split_axis=0, concat_axis=0, tiled=True
+    )
+    total = both(both(total, "zh"), "x")
+    scale = jnp.float32(local * devices) / total
     mixed, token_grad, gate_grad = call(
-        functools.partial(unpack_kernel, float(local * devices)),
-        [SM, VM, VM, VM, VM],
+        unpack_kernel,
+        [SM, SM, VM, VM, VM, VM],
         [VM, VM, VM],
         [
             jax.ShapeDtypeStruct((local, units), BF),
@@ -262,7 +256,7 @@
         ],
         "unpack",
         2 * rows * local * 2 * wide,
-    )(counts, route, gate, home.reshape(rows, wide + LANES), cotangent)
+    )(counts, scale, route, gate, home.reshape(rows, wide), cotangent)
     return (mixed, token_grad, gate_grad.reshape(local, 1))
 
 

time: 140 us -> 165 us (1.18)
  the two profiles are of different devices: /device:TPU:1 before, /device:TPU:366 now
where the time goes in v4:
time: 165 us; the launch traced here: 164 us
  waiting for transfers between devices  67.8 us (41%)
  starting transfers between devices  60.5 us (37%)
  blocking collectives  14.7 us (9%)
  Pallas kernels  14.1 us (9%)
  between operations  7.03 us (4%)
    ppermute x7, waiting for transfers between devices, both(): lax.ppermute(value, axis, [(i, i ^ apart) for i in range(size)])  63.8 us
    ppermute x7, starting transfers between devices, both(): lax.ppermute(value, axis, [(i, i ^ apart) for i in range(size)])  27.1 us
    all_to_all x1, starting transfers between devices, shards(): lax.all_to_all(payload.reshape(experts, ROWS, wide), group, split_axis=0,...  17.6 us
    all_to_all x1, starting transfers between devices, shards(): lax.all_to_all(back.reshape(experts, ROWS, wide), group, split_axis=0, co...  15.7 us
    psum x1, blocking collectives, shards(): total = both(both(lax.psum(counts.astype(F32), 'y'), 'zl'), 'core')  14.7 us
    pallas_call x1, Pallas kernels, shards(): call(expert_kernel, [SM, VM, HB], [VM, SM], [jax.ShapeDtypeStruct((rows,...  8.72 us
    all_to_all x1, waiting for transfers between devices, shards(): lax.all_to_all(payload.reshape(experts, ROWS, wide), group, split_axis=0,...  4.07 us
    pallas_call x1, Pallas kernels, shards(): call(pack_kernel, [SM, HB, HB, HB, HB], HB, jax.ShapeDtypeStruct((rows, w...  3.49 us
  transfers between devices with their start and end apart: 9, of which 8 were waited for; matrix products, arithmetic and copies ran while one was open for 0% of the time, Pallas kernels for 0%

profile of v4, /device:TPU:366, one launch (start us, length us, event | category | flops | bytes accessed | tf_op | source)
XLA Modules:
  0.0 164.1 jit_solution(9330384177911937074)
XLA Ops:
  1.3 3.5 %pack.1 = bf16[256,3456]{1,0:T(8,128)(2,1)} custom-call(s32[1]{0:T(128)S(6)} %copy.9.count, s32[1,128]{1,0:T(1,128)} %bitcast.10, f32[1,128]{1,0:T(1,128)} %bitcast.12, bf16[128,3584]{1,0:T(8,128)(2,1)} %tokens_in.1, bf16[128,1024]{1,0:T(8,128)(2,1)} %cotangent.1), custom_call_target="tpu_custom_call" | custom-call | flops 452984832 | bytes 10000000 | tf_op jit(solution)/shard_map/pack/pallas_call | solution.py:212
  4.8 17.6 %all-to-all-start = ((bf16[32,8,3456]{2,1,0:T(8,128)(2,1)}), bf16[32,8,3456]{2,1,0:T(8,128)(2,1)S(1)}, u32[]{:S(2)}, u32[]{:S(2)}) async-start(bf16[32,8,3456]{2,1,0:T(8,128)(2,1)} %bitcast.14), calls=%async_computation | async-start | bytes 3538944 | tf_op jit(solution)/shard_map/all_to_all | solution.py:229
  22.4 14.7 %psum.7 = f32[1]{0:T(128)} all-reduce(f32[1]{0:T(128)S(6)} %convert_element_type.3), channel_id=1, replica_groups=mesh['y'=8,'zl'=4,'x'=8,'zh'=2,'core'=2] {'y'}, use_global_device_ids=true, to_apply=%region_0.0 | all-reduce | flops 1 | bytes 8 | tf_op jit(solution)/shard_map/psum | solution.py:232
  37.1 4.3 %collective-permute-start = (f32[1]{0:T(128)}, f32[1]{0:T(128)}, u32[]{:S(2)}, u32[]{:S(2)}) collective-permute-start(f32[1]{0:T(128)} %psum.7), channel_id=1, source_target_pairs={{0,32},{32,0},{64,96},{96,64},{1,33},{33,1},{65,97},{97,65},{2,34}... | collective-permute-start | bytes 20 | tf_op jit(solution)/shard_map/ppermute | solution.py:196
  41.4 9.9 %collective-permute-done = f32[1]{0:T(128)} collective-permute-done((f32[1]{0:T(128)}, f32[1]{0:T(128)}, u32[]{:S(2)}, u32[]{:S(2)}) %collective-permute-start) | collective-permute-done | bytes 36 | tf_op jit(solution)/shard_map/ppermute | solution.py:196
  52.6 3.2 %collective-permute-start.1 = (f32[1]{0:T(128)}, f32[1]{0:T(128)}, u32[]{:S(2)}, u32[]{:S(2)}) collective-permute-start(f32[1]{0:T(128)} %add.23), channel_id=1, source_target_pairs={{0,64},{32,96},{64,0},{96,32},{1,65},{33,97},{65,1},{97,33},{2,66}... | collective-permute-start | bytes 20 | tf_op jit(solution)/shard_map/ppermute | solution.py:196
  55.8 3.1 %collective-permute-done.1 = f32[1]{0:T(128)} collective-permute-done((f32[1]{0:T(128)}, f32[1]{0:T(128)}, u32[]{:S(2)}, u32[]{:S(2)}) %collective-permute-start.1) | collective-permute-done | bytes 36 | tf_op jit(solution)/shard_map/ppermute | solution.py:196
  59.5 2.7 %collective-permute-start.2 = (f32[1]{0:T(128)}, f32[1]{0:T(128)}, u32[]{:S(2)}, u32[]{:S(2)}) collective-permute-start(f32[1]{0:T(128)} %add.24), channel_id=1, source_target_pairs={{0,1},{1,0},{2,3},{3,2},{4,5},{5,4},{6,7},{7,6},{8,9},{9,8},{10,11... | collective-permute-start | bytes 20 | tf_op jit(solution)/shard_map/ppermute | solution.py:196
  62.3 0.3 collective-permute-done.2
  63.2 4.1 %all-to-all-done = bf16[32,8,3456]{2,1,0:T(8,128)(2,1)S(1)} async-done(((bf16[32,8,3456]{2,1,0:T(8,128)(2,1)}), bf16[32,8,3456]{2,1,0:T(8,128)(2,1)S(1)}, u32[]{:S(2)}, u32[]{:S(2)}) %all-to-all-start) | async-done | bytes 1769504 | tf_op jit(solution)/shard_map/all_to_all | solution.py:229
  67.2 8.7 %expert.1 = (bf16[256,3456]{1,0:T(8,128)(2,1)}, f32[1]{0:T(128)}) custom-call(f32[1]{0:T(128)S(6)} %add.25.total, bf16[256,3456]{1,0:T(8,128)(2,1)S(1)} %bitcast.9, bf16[3584,1024]{1,0:T(8,128)(2,1)} %bitcast.15), custom_call_target="tpu_custom_call" | custom-call | flops 3758096384 | bytes 10000000 | tf_op jit(solution)/shard_map/expert/pallas_call | solution.py:233
  76.0 0.0 copy-start
  76.0 0.0 copy-start.1
  76.0 0.0 copy-start.2
  76.0 15.7 %all-to-all-start.1 = ((bf16[32,8,3456]{2,1,0:T(8,128)(2,1)}), bf16[32,8,3456]{2,1,0:T(8,128)(2,1)S(1)}, u32[]{:S(2)}, u32[]{:S(2)}) async-start(bf16[32,8,3456]{2,1,0:T(8,128)(2,1)} %bitcast.5), calls=%async_computation.1 | async-start | bytes 3538944 | tf_op jit(solution)/shard_map/all_to_all | solution.py:243
  91.8 7.3 %collective-permute-start.3 = (f32[1]{0:T(128)}, f32[1]{0:T(128)}, u32[]{:S(2)}, u32[]{:S(2)}) collective-permute-start(f32[1]{0:T(128)} %get-tuple-element.8), channel_id=1, source_target_pairs={{0,2},{2,0},{1,3},{3,1},{4,6},{6,4},{5,7},{7,5},{8,10},{10,8},{9,1... | collective-permute-start | bytes 20 | tf_op jit(solution)/shard_map/ppermute | solution.py:196
  99.1 39.0 %collective-permute-done.3 = f32[1]{0:T(128)} collective-permute-done((f32[1]{0:T(128)}, f32[1]{0:T(128)}, u32[]{:S(2)}, u32[]{:S(2)}) %collective-permute-start.3) | collective-permute-done | bytes 36 | tf_op jit(solution)/shard_map/ppermute | solution.py:196
  139.3 3.2 %collective-permute-start.4 = (f32[1]{0:T(128)}, f32[1]{0:T(128)}, u32[]{:S(2)}, u32[]{:S(2)}) collective-permute-start(f32[1]{0:T(128)} %add.26), channel_id=1, source_target_pairs={{0,4},{4,0},{8,12},{12,8},{16,20},{20,16},{24,28},{28,24},{1,5},{5... | collective-permute-start | bytes 20 | tf_op jit(solution)/shard_map/ppermute | solution.py:196
  142.5 2.2 %collective-permute-done.4 = f32[1]{0:T(128)} collective-permute-done((f32[1]{0:T(128)}, f32[1]{0:T(128)}, u32[]{:S(2)}, u32[]{:S(2)}) %collective-permute-start.4) | collective-permute-done | bytes 36 | tf_op jit(solution)/shard_map/ppermute | solution.py:196
  145.3 3.2 %collective-permute-start.5 = (f32[1]{0:T(128)}, f32[1]{0:T(128)}, u32[]{:S(2)}, u32[]{:S(2)}) collective-permute-start(f32[1]{0:T(128)} %add.27), channel_id=1, source_target_pairs={{0,8},{4,12},{8,0},{12,4},{16,24},{20,28},{24,16},{28,20},{1,9},{5... | collective-permute-start | bytes 20 | tf_op jit(solution)/shard_map/ppermute | solution.py:196
  148.5 3.1 %collective-permute-done.5 = f32[1]{0:T(128)} collective-permute-done((f32[1]{0:T(128)}, f32[1]{0:T(128)}, u32[]{:S(2)}, u32[]{:S(2)}) %collective-permute-start.5) | collective-permute-done | bytes 36 | tf_op jit(solution)/shard_map/ppermute | solution.py:196
  152.2 3.2 %collective-permute-start.6 = (f32[1]{0:T(128)}, f32[1]{0:T(128)}, u32[]{:S(2)}, u32[]{:S(2)}) collective-permute-start(f32[1]{0:T(128)} %add.28), channel_id=1, source_target_pairs={{0,16},{4,20},{8,24},{12,28},{16,0},{20,4},{24,8},{28,12},{1,17},{... | collective-permute-start | bytes 20 | tf_op jit(solution)/shard_map/ppermute | solution.py:196
  155.4 6.1 %collective-permute-done.6 = f32[1]{0:T(128)} collective-permute-done((f32[1]{0:T(128)}, f32[1]{0:T(128)}, u32[]{:S(2)}, u32[]{:S(2)}) %collective-permute-start.6) | collective-permute-done | bytes 36 | tf_op jit(solution)/shard_map/ppermute | solution.py:196
  162.2 0.0 all-to-all-done.1
  162.2 0.0 copy-done
  162.2 0.0 copy-done.1
  162.2 0.0 copy-done.2
  162.2 1.9 %unpack.1 = (bf16[128,1024]{1,0:T(8,128)(2,1)}, bf16[128,3584]{1,0:T(8,128)(2,1)}, f32[1,128]{1,0:T(1,128)}) custom-call(s32[1]{0:T(128)S(6)} %copy.9.count, f32[1]{0:T(128)S(6)} %div.3.scale_in, s32[1,128]{1,0:T(1,128)S(1)} %bitcast.11, f32[1,128]{1,0:T(1,128)S(1)} %bitcast.13, bf16[256,3456]{1,0:T(8,128)(2,1)S(1)} %bitcast.8, bf16[128,1024]{1,0:T(8,128)(2,1)S(1)} %copy-done), custom_call_target="tpu_custom_call" | custom-call | flops 452984832 | bytes 10000000 | tf_op jit(solution)/shard_map/unpack/pallas_call | solution.py:248
Async XLA Ops:
  4.8 62.5 %all-to-all-start = ((bf16[32,8,3456]{2,1,0:T(8,128)(2,1)}), bf16[32,8,3456]{2,1,0:T(8,128)(2,1)S(1)}, u32[]{:S(2)}, u32[]{:S(2)}) async-start(bf16[32,8,3456]{2,1,0:T(8,128)(2,1)} %bitcast.14), calls=%async_computation | async-start | bytes 3538944 | tf_op jit(solution)/shard_map/all_to_all | solution.py:229
  37.1 14.2 %collective-permute-start = (f32[1]{0:T(128)}, f32[1]{0:T(128)}, u32[]{:S(2)}, u32[]{:S(2)}) collective-permute-start(f32[1]{0:T(128)} %psum.7), channel_id=1, source_target_pairs={{0,32},{32,0},{64,96},{96,64},{1,33},{33,1},{65,97},{97,65},{2,34}... | collective-permute-start | bytes 20 | tf_op jit(solution)/shard_map/ppermute | solution.py:196
  52.6 6.3 %collective-permute-start.1 = (f32[1]{0:T(128)}, f32[1]{0:T(128)}, u32[]{:S(2)}, u32[]{:S(2)}) collective-permute-start(f32[1]{0:T(128)} %add.23), channel_id=1, source_target_pairs={{0,64},{32,96},{64,0},{96,32},{1,65},{33,97},{65,1},{97,33},{2,66}... | collective-permute-start | bytes 20 | tf_op jit(solution)/shard_map/ppermute | solution.py:196
  59.5 3.0 %collective-permute-start.2 = (f32[1]{0:T(128)}, f32[1]{0:T(128)}, u32[]{:S(2)}, u32[]{:S(2)}) collective-permute-start(f32[1]{0:T(128)} %add.24), channel_id=1, source_target_pairs={{0,1},{1,0},{2,3},{3,2},{4,5},{5,4},{6,7},{7,6},{8,9},{9,8},{10,11... | collective-permute-start | bytes 20 | tf_op jit(solution)/shard_map/ppermute | solution.py:196
  76.0 86.2 %copy-start = (bf16[128,1024]{1,0:T(8,128)(2,1)S(1)}, bf16[128,1024]{1,0:T(8,128)(2,1)}, u32[]{:S(2)}) copy-start(bf16[128,1024]{1,0:T(8,128)(2,1)} %cotangent.1) | copy-start | bytes 786436
  76.0 86.2 %copy-start.1 = (s32[128,1]{0,1:T(1,128)S(1)}, s32[128,1]{0,1:T(1,128)}, u32[]{:S(2)}) copy-start(s32[128,1]{0,1:T(1,128)} %param.7) | copy-start | bytes 1540
  76.0 86.2 %copy-start.2 = (f32[128,1]{0,1:T(1,128)S(1)}, f32[128,1]{0,1:T(1,128)}, u32[]{:S(2)}) copy-start(f32[128,1]{0,1:T(1,128)} %param.8) | copy-start | bytes 1540
  76.0 86.2 %all-to-all-start.1 = ((bf16[32,8,3456]{2,1,0:T(8,128)(2,1)}), bf16[32,8,3456]{2,1,0:T(8,128)(2,1)S(1)}, u32[]{:S(2)}, u32[]{:S(2)}) async-start(bf16[32,8,3456]{2,1,0:T(8,128)(2,1)} %bitcast.5), calls=%async_computation.1 | async-start | bytes 3538944 | tf_op jit(solution)/shard_map/all_to_all | solution.py:243
  91.8 46.3 %collective-permute-start.3 = (f32[1]{0:T(128)}, f32[1]{0:T(128)}, u32[]{:S(2)}, u32[]{:S(2)}) collective-permute-start(f32[1]{0:T(128)} %get-tuple-element.8), channel_id=1, source_target_pairs={{0,2},{2,0},{1,3},{3,1},{4,6},{6,4},{5,7},{7,5},{8,10},{10,8},{9,1... | collective-permute-start | bytes 20 | tf_op jit(solution)/shard_map/ppermute | solution.py:196
  139.3 5.4 %collective-permute-start.4 = (f32[1]{0:T(128)}, f32[1]{0:T(128)}, u32[]{:S(2)}, u32[]{:S(2)}) collective-permute-start(f32[1]{0:T(128)} %add.26), channel_id=1, source_target_pairs={{0,4},{4,0},{8,12},{12,8},{16,20},{20,16},{24,28},{28,24},{1,5},{5... | collective-permute-start | bytes 20 | tf_op jit(solution)/shard_map/ppermute | solution.py:196
  145.3 6.3 %collective-permute-start.5 = (f32[1]{0:T(128)}, f32[1]{0:T(128)}, u32[]{:S(2)}, u32[]{:S(2)}) collective-permute-start(f32[1]{0:T(128)} %add.27), channel_id=1, source_target_pairs={{0,8},{4,12},{8,0},{12,4},{16,24},{20,28},{24,16},{28,20},{1,9},{5... | collective-permute-start | bytes 20 | tf_op jit(solution)/shard_map/ppermute | solution.py:196
  152.2 9.3 %collective-permute-start.6 = (f32[1]{0:T(128)}, f32[1]{0:T(128)}, u32[]{:S(2)}, u32[]{:S(2)}) collective-permute-start(f32[1]{0:T(128)} %add.28), channel_id=1, source_target_pairs={{0,16},{4,20},{8,24},{12,28},{16,0},{20,4},{24,8},{28,12},{1,17},{... | collective-permute-start | bytes 20 | tf_op jit(solution)/shard_map/ppermute | solution.py:196

commit v5 on v3

--- a/solution.py
+++ b/solution.py
@@ -28,7 +28,12 @@
     return lax.broadcasted_iota(jnp.int32, shape, axis)
 
 
+def turned_order(index, experts):
+    return jnp.bitwise_and(3 * jnp.right_shift(index, 2), experts // 4 - 1) * 4 + jnp.bitwise_and(index, 3)
+
+
 def places(route, experts):
+    route = turned_order(route, experts)
     tokens = route.shape[1]
     choose = (iota((experts, tokens), 0) == route).astype(F32)
     before = (iota((tokens, tokens), 0) < iota((tokens, tokens), 1)).astype(BF)
@@ -208,6 +213,7 @@
     experts = lax.axis_size("x") * lax.axis_size("zh") * lax.axis_size("core")
     devices = experts * lax.axis_size("y") * lax.axis_size("zl")
     group = ("x", "zh", "core")
+    order = [[(3 * (i // 4)) % (experts // 4) * 4 + i % 4 for i in range(experts)]]
     rows = experts * ROWS
     wide = (deep + units) * SLOTS // ROWS
     route = routes.reshape(1, local)
@@ -231,7 +237,8 @@
         room=67_043_328,
     )(counts, route, gate, tokens, cotangent)
     arrived = lax.all_to_all(
-        payload.reshape(experts, ROWS, wide), group, split_axis=0, concat_axis=0, tiled=True
+        payload.reshape(experts, ROWS, wide), group, split_axis=0, concat_axis=0, tiled=True,
+        axis_index_groups=order
     )
     total = lax.psum(counts.astype(F32), "y")
     size, apart = lax.axis_size("zl"), 1
@@ -249,7 +256,8 @@
         room=EXPERT_ROOM,
     )(total, arrived.reshape(rows, wide), weight)
     home = lax.all_to_all(
-        back.reshape(experts, ROWS, wide + LANES), group, split_axis=0, concat_axis=0, tiled=True
+        back.reshape(experts, ROWS, wide + LANES), group, split_axis=0, concat_axis=0, tiled=True,
+        axis_index_groups=order
     )
     mixed, token_grad, gate_grad = call(
         functools.partial(unpack_kernel, float(local * devices)),

time: 140 us -> 141 us (level)
  blocking collectives: 74.3 us -> 77 us
  starting transfers between devices: 33.7 us -> 31 us
    all_to_all x1, blocking collectives: 58.9 us -> 61.6 us  [shards(): lax.all_to_all(back.reshape(experts, ROWS, wide + LANES), group, split_ax...]
    ppermute x2, starting transfers between devices: 13.2 us -> 10.5 us  [shards(): lax.ppermute(total, 'zl', [(i, i ^ apart) for i in range(size)])]
where the time goes in v5:
time: 141 us; the launch traced here: 140 us
  blocking collectives  77 us (55%)
  starting transfers between devices  31 us (22%)
  waiting for transfers between devices  16.1 us (11%)
  Pallas kernels  12.8 us (9%)
  between operations  3.37 us (2%)
    all_to_all x1, blocking collectives, shards(): lax.all_to_all(back.reshape(experts, ROWS, wide + LANES), group, split_ax...  61.6 us
    all_to_all x1, starting transfers between devices, shards(): lax.all_to_all(payload.reshape(experts, ROWS, wide), group, split_axis=0,...  20.5 us
    psum x1, blocking collectives, shards(): total = lax.psum(counts.astype(F32), 'y')  15.5 us
    all_to_all x1, waiting for transfers between devices, shards(): lax.all_to_all(payload.reshape(experts, ROWS, wide), group, split_axis=0,...  14.3 us
    ppermute x2, starting transfers between devices, shards(): lax.ppermute(total, 'zl', [(i, i ^ apart) for i in range(size)])  10.5 us
    pallas_call x1, Pallas kernels, shards(): call(expert_kernel, [SM, VM, HB], VM, jax.ShapeDtypeStruct((rows, wide +...  7.36 us
    pallas_call x1, Pallas kernels, shards(): call(pack_kernel, [SM, HB, HB, HB, HB], HB, jax.ShapeDtypeStruct((rows, w...  3.51 us
  transfers between devices with their start and end apart: 3, of which 3 were waited for; matrix products, arithmetic and copies ran while one was open for 0% of the time, Pallas kernels for 0%

profile of v5, /device:TPU:1, one launch (start us, length us, event | category | flops | bytes accessed | tf_op | source)
XLA Modules:
  0.0 140.3 jit_solution(12297182772937987035)
XLA Ops:
  1.3 3.5 %pack.1 = bf16[256,3456]{1,0:T(8,128)(2,1)} custom-call(s32[1]{0:T(128)S(6)} %copy.9.count, s32[1,128]{1,0:T(1,128)} %bitcast.11, f32[1,128]{1,0:T(1,128)} %bitcast.13, bf16[128,3584]{1,0:T(8,128)(2,1)} %tokens_in.1, bf16[128,1024]{1,0:T(8,128)(2,1)} %cotangent.1), custom_call_target="tpu_custom_call" | custom-call | flops 452984832 | bytes 10000000 | tf_op jit(solution)/shard_map/pack/pallas_call | solution.py:222
  4.8 20.5 %all-to-all-start = ((bf16[32,8,3456]{2,1,0:T(8,128)(2,1)}), bf16[32,8,3456]{2,1,0:T(8,128)(2,1)S(1)}, u32[]{:S(2)}, u32[]{:S(2)}) async-start(bf16[32,8,3456]{2,1,0:T(8,128)(2,1)} %bitcast.15), calls=%async_computation | async-start | bytes 3538944 | tf_op jit(solution)/shard_map/all_to_all | solution.py:239
  25.3 15.5 %psum.7 = f32[1]{0:T(128)} all-reduce(f32[1]{0:T(128)S(6)} %convert_element_type.3), channel_id=1, replica_groups=mesh['y'=8,'zl'=4,'x'=8,'zh'=2,'core'=2] {'y'}, use_global_device_ids=true, to_apply=%region_0.0 | all-reduce | flops 1 | bytes 8 | tf_op jit(solution)/shard_map/psum | solution.py:243
  40.8 4.0 %collective-permute-start = (f32[1]{0:T(128)}, f32[1]{0:T(128)}, u32[]{:S(2)}, u32[]{:S(2)}) collective-permute-start(f32[1]{0:T(128)} %psum.7), channel_id=1, source_target_pairs={{0,32},{32,0},{64,96},{96,64},{1,33},{33,1},{65,97},{97,65},{2,34}... | collective-permute-start | bytes 20 | tf_op jit(solution)/shard_map/ppermute | solution.py:246
  44.8 1.4 %collective-permute-done = f32[1]{0:T(128)} collective-permute-done((f32[1]{0:T(128)}, f32[1]{0:T(128)}, u32[]{:S(2)}, u32[]{:S(2)}) %collective-permute-start) | collective-permute-done | bytes 36 | tf_op jit(solution)/shard_map/ppermute | solution.py:246
  47.5 6.5 %collective-permute-start.1 = (f32[1]{0:T(128)}, f32[1]{0:T(128)}, u32[]{:S(2)}, u32[]{:S(2)}) collective-permute-start(f32[1]{0:T(128)} %add.8), channel_id=1, source_target_pairs={{0,64},{32,96},{64,0},{96,32},{1,65},{33,97},{65,1},{97,33},{2,66}... | collective-permute-start | bytes 20 | tf_op jit(solution)/shard_map/ppermute | solution.py:246
  54.1 0.4 collective-permute-done.1
  55.2 14.3 %all-to-all-done = bf16[32,8,3456]{2,1,0:T(8,128)(2,1)S(1)} async-done(((bf16[32,8,3456]{2,1,0:T(8,128)(2,1)}), bf16[32,8,3456]{2,1,0:T(8,128)(2,1)S(1)}, u32[]{:S(2)}, u32[]{:S(2)}) %all-to-all-start) | async-done | bytes 1769504 | tf_op jit(solution)/shard_map/all_to_all | solution.py:239
  69.5 7.4 %expert.1 = bf16[256,3584]{1,0:T(8,128)(2,1)S(1)} custom-call(f32[1]{0:T(128)S(6)} %add.9.total, bf16[256,3456]{1,0:T(8,128)(2,1)S(1)} %bitcast.10, bf16[3584,1024]{1,0:T(8,128)(2,1)} %bitcast.16), custom_call_target="tpu_custom_call" | custom-call | flops 3758096384 | bytes 10000000 | tf_op jit(solution)/shard_map/expert/pallas_call | solution.py:248
  76.8 0.0 copy-start
  76.8 0.0 copy-start.1
  76.8 0.0 copy-start.2
  76.9 61.6 %all_to_all.10 = bf16[32,8,3584]{2,1,0:T(8,128)(2,1)S(1)} all-to-all(bf16[32,8,3584]{2,1,0:T(8,128)(2,1)S(1)} %bitcast.9), channel_id=1, replica_groups={{0,1,2,3,12,13,14,15,24,25,26,27,4,5,6,7,16,17,18,19,28,29,30,31,8,9,10..., dimensions={0} | all-to-all | bytes 3670016 | tf_op jit(solution)/shard_map/all_to_all | solution.py:258
  138.4 0.0 copy-done
  138.4 0.0 copy-done.1
  138.4 0.0 copy-done.2
  138.4 1.9 %unpack.1 = (bf16[128,1024]{1,0:T(8,128)(2,1)}, bf16[128,3584]{1,0:T(8,128)(2,1)}, f32[1,128]{1,0:T(1,128)}) custom-call(s32[1]{0:T(128)S(6)} %copy.9.count, s32[1,128]{1,0:T(1,128)S(1)} %bitcast.12, f32[1,128]{1,0:T(1,128)S(1)} %bitcast.14, bf16[256,3584]{1,0:T(8,128)(2,1)S(1)} %bitcast.8, bf16[128,1024]{1,0:T(8,128)(2,1)S(1)} %copy-done), custom_call_target="tpu_custom_call" | custom-call | flops 452984832 | bytes 10000000 | tf_op jit(solution)/shard_map/unpack/pallas_call | solution.py:262
Async XLA Ops:
  4.8 64.7 %all-to-all-start = ((bf16[32,8,3456]{2,1,0:T(8,128)(2,1)}), bf16[32,8,3456]{2,1,0:T(8,128)(2,1)S(1)}, u32[]{:S(2)}, u32[]{:S(2)}) async-start(bf16[32,8,3456]{2,1,0:T(8,128)(2,1)} %bitcast.15), calls=%async_computation | async-start | bytes 3538944 | tf_op jit(solution)/shard_map/all_to_all | solution.py:239
  40.8 5.4 %collective-permute-start = (f32[1]{0:T(128)}, f32[1]{0:T(128)}, u32[]{:S(2)}, u32[]{:S(2)}) collective-permute-start(f32[1]{0:T(128)} %psum.7), channel_id=1, source_target_pairs={{0,32},{32,0},{64,96},{96,64},{1,33},{33,1},{65,97},{97,65},{2,34}... | collective-permute-start | bytes 20 | tf_op jit(solution)/shard_map/ppermute | solution.py:246
  47.5 6.9 %collective-permute-start.1 = (f32[1]{0:T(128)}, f32[1]{0:T(128)}, u32[]{:S(2)}, u32[]{:S(2)}) collective-permute-start(f32[1]{0:T(128)} %add.8), channel_id=1, source_target_pairs={{0,64},{32,96},{64,0},{96,32},{1,65},{33,97},{65,1},{97,33},{2,66}... | collective-permute-start | bytes 20 | tf_op jit(solution)/shard_map/ppermute | solution.py:246
  76.8 61.6 %copy-start = (bf16[128,1024]{1,0:T(8,128)(2,1)S(1)}, bf16[128,1024]{1,0:T(8,128)(2,1)}, u32[]{:S(2)}) copy-start(bf16[128,1024]{1,0:T(8,128)(2,1)} %cotangent.1) | copy-start | bytes 786436
  76.8 61.6 %copy-start.1 = (s32[128,1]{0,1:T(1,128)S(1)}, s32[128,1]{0,1:T(1,128)}, u32[]{:S(2)}) copy-start(s32[128,1]{0,1:T(1,128)} %param.7) | copy-start | bytes 1540
  76.8 61.6 %copy-start.2 = (f32[128,1]{0,1:T(1,128)S(1)}, f32[128,1]{0,1:T(1,128)}, u32[]{:S(2)}) copy-start(f32[128,1]{0,1:T(1,128)} %param.8) | copy-start | bytes 1540
